TPU v7x, 32 devices: a whole 2x2x4 slice. The times are simulated.
32 devices in a mesh: dp: 8 (over y, x, core), seq: 4 (over z).
Axes of the slice: x: 2, y: 2, z: 4, core: 2. Of those that a mesh axis runs over, the one named last changes fastest.
Arguments:
- hidden_in: bfloat16 [8, 2048, 1024], P('dp', 'seq'), may hold values from -6 to 6
- doc_lengths: int32 [8, 8], P('dp'), may hold values from 1 to 1024, 2048 in all within a row
- ln1_gain: float32 [1024], replicated, may hold values from 0.1 to 1.9
- ln1_bias: float32 [1024], replicated, may hold values from -1.75 to 1.75
- ln2_gain: float32 [1024], replicated, may hold values from 0.1 to 1.9
- ln2_bias: float32 [1024], replicated, may hold values from -1.75 to 1.75
- qkv_weight: bfloat16 [1024, 3072], replicated, may hold values from -0.1875 to 0.1875
- qkv_bias: float32 [3072], replicated, may hold values from -1.75 to 1.75
- dense_weight: bfloat16 [1024, 1024], replicated, may hold values from -0.75 to 0.75
- dense_bias: float32 [1024], replicated, may hold values from -1.75 to 1.75
- fc_in_weight: bfloat16 [1024, 4096], replicated, may hold values from -0.1875 to 0.1875
- fc_in_bias: float32 [4096], replicated, may hold values from -1.75 to 1.75
- fc_out_weight: bfloat16 [4096, 1024], replicated, may hold values from -0.09375 to 0.09375
- fc_out_bias: float32 [1024], replicated, may hold values from -1.75 to 1.75
- out_grad: bfloat16 [8, 2048, 1024], P('dp', 'seq'), may hold values from -8 to 8
Outputs:
- hidden_out: bfloat16 [8, 2048, 1024], P('dp', 'seq')
- grad_in: float32 [8, 2048, 1024], P('dp', 'seq')
- grad_ln1_gain: float32 [1024], P(('dp', 'seq'))
- grad_ln1_bias: float32 [1024], P(('dp', 'seq'))
- grad_ln2_gain: float32 [1024], P(('dp', 'seq'))
- grad_ln2_bias: float32 [1024], P(('dp', 'seq'))
- grad_qkv_weight: float32 [1024, 3072], P(('dp', 'seq'))
- grad_qkv_bias: float32 [3072], P(('dp', 'seq'))
- grad_dense_weight: float32 [1024, 1024], P(('dp', 'seq'))
- grad_dense_bias: float32 [1024], P(('dp', 'seq'))
- grad_fc_in_weight: float32 [1024, 4096], P(('dp', 'seq'))
- grad_fc_in_bias: float32 [4096], P(('dp', 'seq'))
- grad_fc_out_weight: float32 [4096, 1024], P(('dp', 'seq'))
- grad_fc_out_bias: float32 [1024], P(('dp', 'seq'))
Inputs may be any that keep to these rules, and one draw needn't show every extreme that they name: `doc_lengths`: each row sums to 2048; its last entry is the padding document.
All inputs are finite; a program needn't handle non-finite values.
Results may differ from a plain program's by a relative error of at most 0.0097.
Values may be sent and summed in bfloat16 or wider, within the bound.
A program may use at most 256 MiB of HBM per device.

v0:
```python
import jax
import jax.numpy as jnp
from jax import lax
from jax.sharding import PartitionSpec as P

HEADS = 16
HEAD = 64
ROT = 16


epsilon = 1e-05
masked_score = -1e30


def layout(lengths, positions):
    doc_ends = jnp.cumsum(lengths, axis=1)
    starts = doc_ends - lengths
    segment = jnp.sum((positions[None, :, None] >= doc_ends[:, None, :]).astype(jnp.int32), axis=2)
    belongs = segment[:, :, None] == jnp.arange(lengths.shape[1], dtype=jnp.int32)[None, None, :]
    doc_start = jnp.sum(jnp.where(belongs, starts[:, None, :], 0), axis=2)
    return (segment, positions[None, :] - doc_start)


def standardize(values):
    average = jnp.mean(values, axis=-1, keepdims=True)
    centered = values - average
    variance = jnp.mean(centered * centered, axis=-1, keepdims=True)
    inv_std = lax.rsqrt(variance + epsilon)
    return (centered * inv_std, inv_std)


def norm_back(d_normed, unit, inv_std, gain):
    gain_grad = jnp.sum(d_normed * unit, axis=0)
    bias_grad = jnp.sum(d_normed, axis=0)
    d_unit = d_normed * gain
    d_input = inv_std * (
        d_unit
        - jnp.mean(d_unit, axis=-1, keepdims=True)
        - unit * jnp.mean(d_unit * unit, axis=-1, keepdims=True)
    )
    return (d_input, gain_grad, bias_grad)


def rotary_tables(positions):
    half_rot = ROT // 2
    inverse = 10000.0 ** (-(2.0 * jnp.arange(half_rot, dtype=jnp.float32)) / ROT)
    angle = positions.astype(jnp.float32)[:, None] * inverse[None, :]
    return (jnp.cos(angle)[:, None, None, :], jnp.sin(angle)[:, None, None, :])


def rotate(packed, cosine, sine_part):
    half_rot = cosine.shape[-1]
    first_half = packed[..., :half_rot]
    second_half = packed[..., half_rot : 2 * half_rot]
    turned = jnp.concatenate(
        [
            first_half * cosine - second_half * sine_part,
            second_half * cosine + first_half * sine_part,
            packed[..., 2 * half_rot :],
        ],
        axis=-1,
    )
    return jnp.concatenate([turned[..., :2, :], packed[..., 2:, :]], axis=-2)


def exact_gelu(values):
    return jax.nn.gelu(values, approximate=False)


def transpose_dot(left, right):
    return lax.dot_general(
        left, right, (((0,), (0,)), ((), ())), preferred_element_type=jnp.float32
    )


def masked_scores(queries, keys_all, seg_full, first_row, last_row, score_scale):
    scores = (
        jnp.einsum(
            "bqhd,bkhd->bhqk",
            queries[:, first_row:last_row],
            keys_all[:, :last_row],
            preferred_element_type=jnp.float32,
        )
        * score_scale
    )
    query_index = jnp.arange(first_row, last_row, dtype=jnp.int32)
    key_index = jnp.arange(last_row, dtype=jnp.int32)
    allowed = (seg_full[:, first_row:last_row, None] == seg_full[:, None, :last_row]) & (
        query_index[None, :, None] >= key_index[None, None, :]
    )
    return jnp.where(allowed[:, None], scores, masked_score)


def shards(
    hidden_in,
    doc_lengths,
    ln1_gain,
    ln1_bias,
    ln2_gain,
    ln2_bias,
    qkv_weight,
    qkv_bias,
    dense_weight,
    dense_bias,
    fc_in_weight,
    fc_in_bias,
    fc_out_weight,
    fc_out_bias,
    out_grad,
):
    seqs_here, local_len, model_width = hidden_in.shape
    seq_parts = lax.axis_size("seq")
    full_len = local_len * seq_parts
    heads_here = HEADS // seq_parts
    row_count = seqs_here * local_len
    score_scale = HEAD ** (-0.5)
    block_rows = min(512, full_len)
    local_pos = lax.axis_index("seq") * local_len + jnp.arange(local_len, dtype=jnp.int32)
    seg_local, pos_local = layout(doc_lengths, local_pos)
    live_rows = (seg_local < doc_lengths.shape[1] - 1).astype(jnp.float32).reshape(row_count, 1)
    input_f32 = hidden_in.astype(jnp.float32).reshape(row_count, model_width)
    unit_attn, inv_attn = standardize(input_f32)
    unit_mlp, inv_mlp = standardize(input_f32)
    normed_attn = (unit_attn * ln1_gain + ln1_bias).astype(jnp.bfloat16)
    normed_mlp = (unit_mlp * ln2_gain + ln2_bias).astype(jnp.bfloat16)
    qkv_f32 = jnp.dot(normed_attn, qkv_weight, preferred_element_type=jnp.float32) + qkv_bias
    shaped = qkv_f32.reshape(row_count, HEADS, 3, HEAD)
    cosine, sine_part = rotary_tables(pos_local.reshape(row_count))
    turned = (
        rotate(shaped, cosine, sine_part)
        .astype(jnp.bfloat16)
        .reshape(seqs_here, local_len, 3 * model_width)
    )
    head_side = lax.all_to_all(turned, "seq", split_axis=2, concat_axis=1, tiled=True).reshape(
        seqs_here, full_len, heads_here, 3, HEAD
    )
    queries = head_side[:, :, :, 0]
    keys_all = head_side[:, :, :, 1]
    values_all = head_side[:, :, :, 2]
    seg_full, _ = layout(doc_lengths, jnp.arange(full_len, dtype=jnp.int32))
    context_parts = []
    lse_parts = []
    for first_row in range(0, full_len, block_rows):
        last_row = first_row + block_rows
        scores = masked_scores(queries, keys_all, seg_full, first_row, last_row, score_scale)
        peak_score = jnp.max(scores, axis=-1, keepdims=True)
        exponentials = jnp.exp(scores - peak_score)
        weight_sum = jnp.sum(exponentials, axis=-1, keepdims=True)
        probability = exponentials / weight_sum
        lse_parts.append(peak_score[..., 0] + jnp.log(weight_sum[..., 0]))
        context_parts.append(
            jnp.einsum(
                "bhqk,bkhd->bqhd",
                probability.astype(jnp.bfloat16),
                values_all[:, :last_row],
                preferred_element_type=jnp.float32,
            )
        )
    context_heads = (
        jnp.concatenate(context_parts, axis=1)
        .astype(jnp.bfloat16)
        .reshape(seqs_here, full_len, heads_here * HEAD)
    )
    log_sums = jnp.concatenate(lse_parts, axis=2)
    context_tok = lax.all_to_all(
        context_heads, "seq", split_axis=1, concat_axis=2, tiled=True
    ).reshape(row_count, model_width)
    attn_branch = (
        jnp.dot(context_tok, dense_weight, preferred_element_type=jnp.float32) + dense_bias
    )
    pre_act = jnp.dot(normed_mlp, fc_in_weight, preferred_element_type=jnp.float32) + fc_in_bias
    activated, gelu_pull = jax.vjp(exact_gelu, pre_act)
    act_low = activated.astype(jnp.bfloat16)
    mlp_branch = jnp.dot(act_low, fc_out_weight, preferred_element_type=jnp.float32) + fc_out_bias
    hidden_out = (
        (input_f32 + attn_branch + mlp_branch)
        .astype(jnp.bfloat16)
        .reshape(seqs_here, local_len, model_width)
    )
    gradient = out_grad.astype(jnp.float32).reshape(row_count, model_width) * live_rows
    grad_low = gradient.astype(jnp.bfloat16)
    g_dense_w = transpose_dot(context_tok, grad_low)
    g_dense_b = jnp.sum(gradient, axis=0)
    d_context = jnp.dot(grad_low, dense_weight.T, preferred_element_type=jnp.float32).astype(
        jnp.bfloat16
    )
    d_context_heads = lax.all_to_all(
        d_context.reshape(seqs_here, local_len, model_width),
        "seq",
        split_axis=2,
        concat_axis=1,
        tiled=True,
    ).reshape(seqs_here, full_len, heads_here, HEAD)
    g_out_w = transpose_dot(act_low, grad_low)
    g_out_b = jnp.sum(gradient, axis=0)
    d_act = jnp.dot(grad_low, fc_out_weight.T, preferred_element_type=jnp.float32)
    d_pre = gelu_pull(d_act)[0].astype(jnp.bfloat16)
    g_in_w = transpose_dot(normed_mlp, d_pre)
    g_in_b = jnp.sum(d_pre.astype(jnp.float32), axis=0)
    d_mlp_in = jnp.dot(d_pre, fc_in_weight.T, preferred_element_type=jnp.float32)
    d_keys = jnp.zeros((seqs_here, full_len, heads_here, HEAD), jnp.float32)
    d_values = jnp.zeros((seqs_here, full_len, heads_here, HEAD), jnp.float32)
    d_query_parts = []
    for first_row in range(0, full_len, block_rows):
        last_row = first_row + block_rows
        scores = masked_scores(queries, keys_all, seg_full, first_row, last_row, score_scale)
        probability = jnp.exp(scores - log_sums[:, :, first_row:last_row, None])
        grad_rows = d_context_heads[:, first_row:last_row]
        d_values = d_values.at[:, :last_row].add(
            jnp.einsum(
                "bhqk,bqhd->bkhd",
                probability.astype(jnp.bfloat16),
                grad_rows,
                preferred_element_type=jnp.float32,
            )
        )
        d_prob = jnp.einsum(
            "bqhd,bkhd->bhqk",
            grad_rows,
            values_all[:, :last_row],
            preferred_element_type=jnp.float32,
        )
        row_delta = jnp.sum(probability * d_prob, axis=-1, keepdims=True)
        d_scores = (probability * (d_prob - row_delta)).astype(jnp.bfloat16)
        d_query_parts.append(
            jnp.einsum(
                "bhqk,bkhd->bqhd",
                d_scores,
                keys_all[:, :last_row],
                preferred_element_type=jnp.float32,
            )
            * score_scale
        )
        d_keys = d_keys.at[:, :last_row].add(
            jnp.einsum(
                "bhqk,bqhd->bkhd",
                d_scores,
                queries[:, first_row:last_row],
                preferred_element_type=jnp.float32,
            )
            * score_scale
        )
    d_queries = jnp.concatenate(d_query_parts, axis=1)
    d_heads = (
        jnp.stack([d_queries, d_keys, d_values], axis=3)
        .astype(jnp.bfloat16)
        .reshape(seqs_here, full_len, heads_here * 3 * HEAD)
    )
    d_tokens = lax.all_to_all(d_heads, "seq", split_axis=1, concat_axis=2, tiled=True).reshape(
        row_count, HEADS, 3, HEAD
    )
    _, rotate_pull = jax.vjp(lambda packed: rotate(packed, cosine, sine_part), shaped)
    d_qkv = (
        rotate_pull(d_tokens.astype(jnp.float32))[0]
        .reshape(row_count, 3 * model_width)
        .astype(jnp.bfloat16)
    )
    g_qkv_w = transpose_dot(normed_attn, d_qkv)
    g_qkv_b = jnp.sum(d_qkv.astype(jnp.float32), axis=0)
    d_attn_in = jnp.dot(d_qkv, qkv_weight.T, preferred_element_type=jnp.float32)
    dx_attn, g_gain_one, g_bias_one = norm_back(d_attn_in, unit_attn, inv_attn, ln1_gain)
    dx_mlp, g_gain_two, g_bias_two = norm_back(d_mlp_in, unit_mlp, inv_mlp, ln2_gain)
    grad_in = (gradient + dx_attn + dx_mlp).reshape(seqs_here, local_len, model_width)
    grad_terms = (
        g_gain_one,
        g_bias_one,
        g_gain_two,
        g_bias_two,
        g_qkv_w,
        g_qkv_b,
        g_dense_w,
        g_dense_b,
        g_in_w,
        g_in_b,
        g_out_w,
        g_out_b,
    )
    reduced = (
        lax.psum_scatter(grad_terms[0], ("dp", "seq"), scatter_dimension=0, tiled=True),
        lax.psum_scatter(grad_terms[1], ("dp", "seq"), scatter_dimension=0, tiled=True),
        lax.psum_scatter(grad_terms[2], ("dp", "seq"), scatter_dimension=0, tiled=True),
        lax.psum_scatter(grad_terms[3], ("dp", "seq"), scatter_dimension=0, tiled=True),
        lax.psum_scatter(grad_terms[4], ("dp", "seq"), scatter_dimension=0, tiled=True),
        lax.psum_scatter(grad_terms[5], ("dp", "seq"), scatter_dimension=0, tiled=True),
        lax.psum_scatter(grad_terms[6], ("dp", "seq"), scatter_dimension=0, tiled=True),
        lax.psum_scatter(grad_terms[7], ("dp", "seq"), scatter_dimension=0, tiled=True),
        lax.psum_scatter(grad_terms[8], ("dp", "seq"), scatter_dimension=0, tiled=True),
        lax.psum_scatter(grad_terms[9], ("dp", "seq"), scatter_dimension=0, tiled=True),
        lax.psum_scatter(grad_terms[10], ("dp", "seq"), scatter_dimension=0, tiled=True),
        lax.psum_scatter(grad_terms[11], ("dp", "seq"), scatter_dimension=0, tiled=True),
    )
    return (hidden_out, grad_in) + tuple(reduced)


def solution(mesh):
    return jax.shard_map(
        shards,
        mesh=mesh,
        in_specs=(
            P("dp", "seq", None),
            P("dp", None),
            P(),
            P(),
            P(),
            P(),
            P(),
            P(),
            P(),
            P(),
            P(),
            P(),
            P(),
            P(),
            P("dp", "seq", None),
        ),
        out_specs=(
            P("dp", "seq", None),
            P("dp", "seq", None),
            P(("dp", "seq")),
            P(("dp", "seq")),
            P(("dp", "seq")),
            P(("dp", "seq")),
            P(("dp", "seq"), None),
            P(("dp", "seq")),
            P(("dp", "seq"), None),
            P(("dp", "seq")),
            P(("dp", "seq"), None),
            P(("dp", "seq")),
            P(("dp", "seq"), None),
            P(("dp", "seq")),
        ),
        check_vma=False,
    )
```

profile of v0, /device:TPU:0, one launch (start us, length us, event | category | flops | bytes accessed | tf_op | source)
XLA Modules:
  0.0 1515.9 jit_solution(5117657675731257331)
XLA Ops:
  8.9 3.5 fusion.105
  12.4 6.0 copy.119
  18.9 9.0 reduce.49
  28.0 3.7 reshape.1432
  31.7 6.5 all-to-all-start.2
  39.7 8.3 convolution_add_fusion
  48.0 6.6 copy.107
  54.6 3.3 convert.73
  60.8 27.4 %copy.139 = bf16[1,512,3072]{1,0,2:T(2,128)(2,1)} copy(bf16[1,512,3072]{1,2,0:T(8,128)(2,1)S(1)} %bitcast.395) | data formatting | bytes 6291456 | tf_op jit(solution)/shard_map/convert_element_type | solution.py:131
  88.3 22.0 %reduce.47 = bf16[3072,512]{1,0:T(8,128)(2,1)} reduce(bf16[3072,1,512]{2,1,0:T(2,128)(2,1)} %bitcast.392, bf16[]{:T(256)} %broadcast.808), dimensions={1}, to_apply=%bitcast.380.reduce_sub_computation | reduce | bytes 6291458
  110.2 5.2 reshape.1428
  115.5 5.5 all-to-all-start
  126.7 4.0 reshape.1433
  136.1 55.2 %all-to-all-done = bf16[4,2,196608]{2,1,0:T(2,128)(2,1)} async-done(((bf16[4,2,196608]{2,1,0:T(2,128)(2,1)}), bf16[4,2,196608]{2,1,0:T(2,128)(2,1)}, u32[]{:S(2)}, u32[]{:S(2)}) %all-to-all-start) | async-done | bytes 3145760 | tf_op jit(solution)/shard_map/all_to_all | solution.py:134
  191.3 6.2 reshape.1429
  197.5 3.7 copy.132
  201.2 4.1 copy.109
  205.3 6.2 reshape.1399
  218.5 2.9 multiply_reduce_fusion.3
  234.3 5.0 fusion.129
  239.3 8.3 fusion.177
  247.6 8.1 fusion
  255.7 8.5 fusion.130
  266.2 4.8 multiply_convert_fusion.4
  271.0 2.7 fusion.122
  276.9 4.3 multiply_reduce_fusion.2
  281.2 3.6 fusion.116
  287.8 6.4 multiply_reduce_fusion.1
  294.2 7.8 multiply_convert_fusion.1
  304.1 4.5 multiply_convert_fusion.2
  315.1 12.7 fusion.181
  327.8 12.6 reduce.48
  340.4 3.5 reshape.1430
  343.9 4.3 all-to-all-start.1
  348.2 11.5 multiply_reduce_fusion
  359.7 11.9 multiply_convert_fusion
  371.6 4.7 fusion.133
  379.6 3.8 fusion.70
  383.4 4.4 fusion.48
  387.8 4.0 reshape.1431
  391.8 2.7 copy.133
  396.8 4.8 fusion.139
  402.9 8.4 fusion.71
  413.8 15.7 %copy.125 = bf16[1,2048,768]{2,0,1:T(2,128)(2,1)} copy(bf16[1,2048,768]{1,2,0:T(8,128)(2,1)} %bitcast.397) | data formatting | bytes 6291456 | tf_op jit(solution)/shard_map/convert_element_type | solution.py:246
  429.6 33.3 %reduce.50 = bf16[2048,768]{1,0:T(8,128)(2,1)} reduce(bf16[2048,1,768]{2,1,0:T(2,128)(2,1)} %bitcast.391, bf16[]{:T(256)} %broadcast.808), dimensions={1}, to_apply=%bitcast.316.reduce_sub_computation | reduce | bytes 6291458
  462.9 4.5 reshape.1434
  467.4 119.1 %all_to_all.54 = bf16[4,2,196608]{2,1,0:T(2,128)(2,1)} all-to-all(bf16[4,2,196608]{2,1,0:T(2,128)(2,1)} %reshape.1434), channel_id=1, replica_groups=mesh['dp'=8,'seq'=4] {'seq'}, dimensions={0} | all-to-all | bytes 6291456 | tf_op jit(solution)/shard_map/all_to_all | solution.py:249
  586.5 6.2 reshape.1435
  592.6 3.3 copy.126
  595.9 3.2 convert_bitcast_fusion
  599.1 6.5 copy.127
  607.5 3.6 broadcast_select_fusion
  614.6 6.9 fusion.136
  622.2 28.0 %multiply_convert_fusion.3 = (bf16[512,4096]{1,0:T(8,128)(2,1)}, f32[512,4096]{1,0:T(8,128)}, f32[512,4096]{1,0:T(8,128)}) fusion(f32[4096]{0:T(1024)S(1)} %copy-done.45, bf16[1024,4096]{1,0:T(8,128)(2,1)} %param.45, bf16[1,512,1024]{2,1,0:T(8,128)(2,1)S(1)} %copy-done.13, f32[1024]{0:T(1024)S(1)} %copy-done.49, f32[1024]{0:T(1024)S(1)} %copy-done.41, ...), kind=kOutput, calls=%fused_computation.25 | convolution fusion | flops 4436525056 | bytes 30437376 | tf_op jit(solution)/shard_map/dot_general | solution.py:171
  650.3 14.5 convert_reduce_fusion
  666.7 8.5 fusion.171
  675.4 13.9 fusion.164
  689.4 10.7 fusion.183
  700.1 7.4 fusion.182
  710.0 9.3 fusion.87
  721.9 40.6 %all-reduce.13 = (f32[1024]{0:T(1024)S(1)}, f32[1024]{0:T(1024)S(1)}, f32[1024]{0:T(1024)S(1)}, f32[1024]{0:T(1024)S(1)}, f32[3072]{0:T(1024)S(1)}, /*index=5*/f32[1024]{0:T(1024)S(1)}, f32[4096]{0:T(1024)S(1)}) all-reduce(f32[1024]{0:T(1024)S(1)} %get-tuple-element.128, ...), channel_id=2, replica_groups=mesh['dp'=8,'seq'=4] {'dp','seq'}, use_global_device_ids=true, to_apply=%region_23.24.clone | all-reduce | flops 12288 | bytes 98304
  766.1 11.0 reduce-scatter.5.cloned.1.call-done
  777.1 366.4 %reduce-scatter.9.cloned.1.call-done = f32[32,4096]{1,0:T(8,128)} async-done(((f32[1024,4096]{1,0:T(8,128)}), f32[32,4096]{1,0:T(8,128)}) %reduce-scatter.9.cloned.1.call-update) | async-done | bytes 524304 | tf_op jit(solution)/shard_map/reduce_scatter | solution.py:287
  1143.6 365.0 %reduce-scatter.11.cloned.1.call-done = f32[128,1024]{1,0:T(8,128)} async-done(((f32[4096,1024]{1,0:T(8,128)}), f32[128,1024]{1,0:T(8,128)}) %reduce-scatter.11.cloned.1.call-update) | async-done | bytes 524304 | tf_op jit(solution)/shard_map/reduce_scatter | solution.py:289
  (218 shorter events, 80.5 us)
Async XLA Ops:
  7.2 1.7 copy-start
  12.4 25.9 %copy-start.12 = (bf16[1,512,1024]{2,1,0:T(8,128)(2,1)S(1)}, bf16[1,512,1024]{2,1,0:T(8,128)(2,1)}, u32[]{:S(2)}) copy-start(bf16[1,512,1024]{2,1,0:T(8,128)(2,1)} %param.35) | copy-start | bytes 3145732
  18.9 20.8 %copy-start.42 = (f32[1024]{0:T(1024)S(1)}, f32[1024]{0:T(1024)}, u32[]{:S(2)}) copy-start(f32[1024]{0:T(1024)} %param.37) | copy-start | bytes 12292
  18.9 20.8 %copy-start.46 = (f32[3072]{0:T(1024)S(1)}, f32[3072]{0:T(1024)}, u32[]{:S(2)}) copy-start(f32[3072]{0:T(1024)} %param.42) | copy-start | bytes 36868
  18.9 20.8 %copy-start.47 = (f32[1024]{0:T(1024)S(1)}, f32[1024]{0:T(1024)}, u32[]{:S(2)}) copy-start(f32[1024]{0:T(1024)} %param.38) | copy-start | bytes 12292
  31.7 83.8 %all-to-all-start.2 = ((bf16[4,2,65536]{2,1,0:T(2,128)(2,1)}), bf16[4,2,65536]{2,1,0:T(2,128)(2,1)}, u32[]{:S(2)}, u32[]{:S(2)}) async-start(bf16[4,2,65536]{2,1,0:T(2,128)(2,1)} %reshape.1432), calls=%async_computation.2 | async-start | bytes 2097152 | tf_op jit(solution)/shard_map/all_to_all | solution.py:187
  58.8 1.6 copy-start.31
  58.8 1.6 copy-start.33
  115.5 75.9 %all-to-all-start = ((bf16[4,2,196608]{2,1,0:T(2,128)(2,1)}), bf16[4,2,196608]{2,1,0:T(2,128)(2,1)}, u32[]{:S(2)}, u32[]{:S(2)}) async-start(bf16[4,2,196608]{2,1,0:T(2,128)(2,1)} %reshape.1428), calls=%async_computation | async-start | bytes 6291456 | tf_op jit(solution)/shard_map/all_to_all | solution.py:134
  213.8 11.3 copy-start.14
  213.8 13.4 copy-start.16
  213.8 13.4 copy-start.19
  214.8 3.7 copy-start.3
  218.5 2.9 copy-start.30
  223.2 4.1 copy-start.2
  225.1 2.2 copy-start.29
  229.8 4.5 copy-start.1
  234.3 5.0 copy-start.9
  234.3 5.0 copy-start.26
  266.1 10.7 slice-start.3
  266.2 7.5 copy-start.23
  266.2 10.7 slice-start.4
  271.0 10.2 copy-start.10
  271.0 5.9 copy-start.15
  294.2 9.8 slice-start.5
  294.2 7.8 copy-start.17
  294.2 9.8 slice-start.6
  304.1 4.5 copy-start.6
  304.1 4.5 copy-start.20
  308.6 1.9 copy-start.4
  311.8 1.3 copy-start.7
  343.9 43.9 %all-to-all-start.1 = ((bf16[4,2,65536]{2,1,0:T(2,128)(2,1)}), bf16[4,2,65536]{2,1,0:T(2,128)(2,1)}, u32[]{:S(2)}, u32[]{:S(2)}) async-start(bf16[4,2,65536]{2,1,0:T(2,128)(2,1)} %reshape.1430), calls=%async_computation.1 | async-start | bytes 2097152 | tf_op jit(solution)/shard_map/all_to_all | solution.py:165
  348.1 417.9 %reduce-scatter.7.cloned.1.call-start = ((), (), s32[]{:S(2)}) async-start(), calls=%async_computation.9 | async-start | bytes 4325376 | tf_op jit(solution)/shard_map/reduce_scatter | solution.py:285
  359.7 16.7 %copy-start.18 = (bf16[1,2048,4,64]{1,3,2,0:T(8,128)(2,1)S(1)}, bf16[1,2048,4,64]{1,3,2,0:T(8,128)(2,1)}, u32[]{:S(2)}) copy-start(bf16[1,2048,4,64]{1,3,2,0:T(8,128)(2,1)} %copy-done.16) | copy-start | bytes 3145732
  371.5 4.8 copy-start.5
  371.5 6.9 copy-start.11
  371.6 11.8 slice-start
  376.3 3.3 copy-start.8
  376.3 7.0 slice-start.1
  379.6 3.8 slice-start.2
  387.8 9.0 copy-start.38
  401.6 375.5 %reduce-scatter.5.cloned.1.call-start = ((), (), s32[]{:S(2)}) async-start(), calls=%async_computation.8 | async-start | bytes 12976128 | tf_op jit(solution)/shard_map/reduce_scatter | solution.py:283
  402.9 8.5 copy-start.21
  599.1 8.3 copy-start.44
  611.1 0.7 copy-start.34
  612.1 2.5 copy-start.13
  612.1 2.5 copy-start.36
  612.1 2.5 copy-start.40
  612.1 2.5 copy-start.43
  612.1 2.5 copy-start.48
  612.9 1.7 copy-start.22
  621.5 0.7 copy-start.45
  621.5 0.7 copy-start.49
  621.5 522.1 %reduce-scatter.9.cloned.1.call-start = ((), (), s32[]{:S(2)}) async-start(), calls=%async_computation.10 | async-start | bytes 17301504 | tf_op jit(solution)/shard_map/reduce_scatter | solution.py:287
  622.2 28.0 %copy-start.27 = (bf16[1,512,1024]{2,1,0:T(8,128)(2,1)S(1)}, bf16[1,512,1024]{2,1,0:T(8,128)(2,1)}, u32[]{:S(2)}) copy-start(bf16[1,512,1024]{2,1,0:T(8,128)(2,1)} %param.49) | copy-start | bytes 3145732
  664.8 2.0 copy-start.55
  675.2 833.4 %reduce-scatter.11.cloned.1.call-start = ((), (), s32[]{:S(2)}) async-start(), calls=%async_computation.11 | async-start | bytes 17301504 | tf_op jit(solution)/shard_map/reduce_scatter | solution.py:289
  689.4 10.7 copy-start.54
  700.1 7.4 copy-start.25
  700.1 7.4 copy-start.50
  700.1 7.5 copy-start.51
  710.0 9.3 copy-start.24
  710.0 9.3 copy-start.28
  763.2 745.9 %copy-start.53 = (f32[32]{0:T(128)}, f32[32]{0:T(128)S(1)}, u32[]{:S(2)}) copy-start(f32[32]{0:T(128)S(1)} %dynamic-slice.67) | copy-start | bytes 388
  (6 other events, 3.8 us)
Sparse Core Ops, SparseCore 0:
  401.8 176.2 reduce-scatter.6
  621.6 155.4 reduce-scatter.4
  780.1 363.4 reduce-scatter.8
  1146.4 362.1 reduce-scatter.10
where the time goes:
time: 1520 us
  waiting for transfers between devices  798 us (52%)
  matrix products  211 us (14%)
  local copies, waits for them, and re-layouts  160 us (11%)
  blocking collectives  160 us (11%)
  other arithmetic  156 us (10%)
  starting transfers between devices  16.6 us (1%)
    reduce_scatter x1, waiting for transfers between devices, shards(): lax.psum_scatter(grad_terms[8], ('dp', 'seq'), scatter_dimension=0, tiled...  366 us
    reduce_scatter x1, waiting for transfers between devices, shards(): lax.psum_scatter(grad_terms[10], ('dp', 'seq'), scatter_dimension=0, tile...  365 us
    all_to_all x1, blocking collectives, shards(): lax.all_to_all(d_heads, 'seq', split_axis=1, concat_axis=2, tiled=True)  119 us
    unnamed x8, other arithmetic  89.7 us
    unnamed x146, local copies, waits for them, and re-layouts  61.3 us
    all_to_all x1, waiting for transfers between devices, shards(): lax.all_to_all(turned, 'seq', split_axis=2, concat_axis=1, tiled=True)  55.2 us
    unnamed x1, blocking collectives  40.6 us
    dot_general x4, matrix products, transpose_dot(): lax.dot_general(left, right, (((0,), (0,)), ((), ())), preferred_element_...  34.1 us
  transfers between devices with their start and end apart: 7, of which 4 were waited for; matrix products, arithmetic and copies ran while one was open for 22% of the time, Pallas kernels for 0%

commit v1 on v0

v1 whole, which is shorter than its diff:
```python
import functools
import math

import jax
import jax.numpy as jnp
from jax import lax
from jax.experimental import pallas as pl
from jax.experimental.pallas import tpu as pltpu
from jax.sharding import PartitionSpec as P

HEADS = 16
HEAD = 64
ROT = 16
DOC_MOST = 1024
EPS = 1e-05
NEG = -1e30
LANES = 128
PAIR = 3 * LANES
BLOCK = 256
F32 = jnp.float32
BF16 = jnp.bfloat16
MIB = 1 << 20


def params(mib=48):
    return pltpu.CompilerParams(vmem_limit_bytes=mib * MIB)


def cost(flops, nbytes, trans=0):
    return pl.CostEstimate(flops=int(flops), bytes_accessed=int(nbytes), transcendentals=int(trans))


def dot(a, b):
    return lax.dot_general(a, b, (((1,), (0,)), ((), ())), preferred_element_type=F32)


def dot_t(a, b):
    return lax.dot_general(a, b, (((1,), (1,)), ((), ())), preferred_element_type=F32)


def whole(shape):
    return pl.BlockSpec(shape, lambda *_: (0,) * len(shape))


def stage_bits(size):
    return [1 << b for b in range(size.bit_length() - 1)]


def stage_order(ndp, nseq, swap):
    dp_bits = stage_bits(ndp)
    if swap and len(dp_bits) > 1:
        dp_bits[-1], dp_bits[-2] = dp_bits[-2], dp_bits[-1]
    return [("dp", b) for b in dp_bits] + [("seq", b) for b in stage_bits(nseq)]


def relative(position, bits):
    out = jnp.zeros_like(position)
    for k, bit in enumerate(bits):
        out = out | jnp.where((position >> (len(bits) - 1 - k)) & 1 == 1, bit, 0)
    return out


def row_sources(rows, stages, ndp, nseq, me_dp, me_seq):
    block = rows // (ndp * nseq)
    i = jnp.arange(rows, dtype=jnp.int32)
    q = i // block
    dp_bits = [b for axis, b in stages if axis == "dp"]
    seq_bits = [b for axis, b in stages if axis == "seq"]
    dest_dp = me_dp ^ relative(q // nseq, dp_bits)
    dest_seq = me_seq ^ relative(q % nseq, seq_bits)
    return ((dest_dp * nseq + dest_seq) * block + i % block).reshape(rows, 1)


def halving(send, keep, stages, sizes):
    got = []
    rows = keep.shape[0]
    for k, (axis, bit) in enumerate(stages):
        if k:
            lo, hi = rows // 2, rows
            total = keep[lo:hi].astype(F32)
            for r in got:
                total = total + r[lo:hi].astype(F32)
            send = total.astype(BF16)
            rows = lo
        got.append(lax.ppermute(send, axis, [(i, i ^ bit) for i in range(sizes[axis])]))
    total = keep[:rows].astype(F32)
    for r in got:
        total = total + r[:rows].astype(F32)
    return total


def unit_of(x):
    mean = jnp.mean(x, axis=-1, keepdims=True)
    c = x - mean
    inv = lax.rsqrt(jnp.mean(c * c, axis=-1, keepdims=True) + EPS)
    return c * inv, inv


def norm_kernel(x_ref, dy_ref, live_ref, g1, b1, g2, b2, a_ref, m_ref, grad_ref, sum_ref):
    u, _ = unit_of(x_ref[...].astype(F32))
    a_ref[...] = (u * g1[...] + b1[...]).astype(BF16)
    m_ref[...] = (u * g2[...] + b2[...]).astype(BF16)
    grad = dy_ref[...].astype(F32) * live_ref[...]
    grad_ref[...] = grad.astype(BF16)

    @pl.when(pl.program_id(0) == 0)
    def _():
        sum_ref[...] = jnp.zeros_like(sum_ref)

    sum_ref[...] += jnp.sum(grad, axis=0, keepdims=True)


def norms(x, dy, live, g1, b1, g2, b2):
    rows, d = x.shape
    tr = 128
    row = pl.BlockSpec((tr, d), lambda i: (i, 0))
    return pl.pallas_call(
        norm_kernel,
        grid=(rows // tr,),
        in_specs=[row, row, pl.BlockSpec((tr, 1), lambda i: (i, 0))] + [whole((1, d))] * 4,
        out_specs=[row, row, row, whole((1, d))],
        out_shape=[jax.ShapeDtypeStruct((rows, d), BF16)] * 3 + [jax.ShapeDtypeStruct((1, d), F32)],
        compiler_params=params(),
        cost_estimate=cost(rows * d * 20, rows * d * 10),
        name="norms",
    )(x, dy, live, g1, b1, g2, b2)


def norm_back_kernel(x_ref, grad_ref, da_ref, db_ref, dm_ref, g1, g2, out_ref, s1g, s1b, s2g, s2b):
    u, inv = unit_of(x_ref[...].astype(F32))
    d1 = da_ref[...] + db_ref[...].astype(F32)
    d2 = dm_ref[...]
    e = d1 * g1[...] + d2 * g2[...]
    dx = inv * (e - jnp.mean(e, axis=-1, keepdims=True) - u * jnp.mean(e * u, axis=-1, keepdims=True))
    out_ref[...] = grad_ref[...].astype(F32) + dx

    @pl.when(pl.program_id(0) == 0)
    def _():
        for s in (s1g, s1b, s2g, s2b):
            s[...] = jnp.zeros_like(s)

    s1g[...] += jnp.sum(d1 * u, axis=0, keepdims=True)
    s1b[...] += jnp.sum(d1, axis=0, keepdims=True)
    s2g[...] += jnp.sum(d2 * u, axis=0, keepdims=True)
    s2b[...] += jnp.sum(d2, axis=0, keepdims=True)


def norm_back(x, grad, d_own, d_got, d_mlp, g1, g2):
    rows, d = x.shape
    tr = 128
    row = pl.BlockSpec((tr, d), lambda i: (i, 0))
    return pl.pallas_call(
        norm_back_kernel,
        grid=(rows // tr,),
        in_specs=[row] * 5 + [whole((1, d))] * 2,
        out_specs=[row] + [whole((1, d))] * 4,
        out_shape=[jax.ShapeDtypeStruct((rows, d), F32)] + [jax.ShapeDtypeStruct((1, d), F32)] * 4,
        compiler_params=params(),
        cost_estimate=cost(rows * d * 30, rows * d * 18),
        name="norm_back",
    )(x, grad, d_own, d_got, d_mlp, g1, g2)


def mlp_kernel(m_ref, grad_ref, win_ref, bin_ref, wout_ref, out_ref, act_ref, dpre_ref, dm_ref, bsum_ref):
    pre = dot(m_ref[...], win_ref[...]) + bin_ref[...]
    cdf = 0.5 * (1.0 + lax.erf(pre * math.sqrt(0.5)))
    act = (pre * cdf).astype(BF16)
    act_ref[...] = act
    d_act = dot_t(grad_ref[...], wout_ref[...])
    slope = cdf + pre * (jnp.exp(-0.5 * pre * pre) * (1.0 / math.sqrt(2.0 * math.pi)))
    d_pre = (d_act * slope).astype(BF16)
    dpre_ref[...] = d_pre
    bsum_ref[...] = jnp.sum(d_pre.astype(F32), axis=0, keepdims=True)

    @pl.when(pl.program_id(0) == 0)
    def _():
        out_ref[...] = jnp.zeros_like(out_ref)
        dm_ref[...] = jnp.zeros_like(dm_ref)

    out_ref[...] += dot(act, wout_ref[...])
    dm_ref[...] += dot_t(d_pre, win_ref[...])


def mlp(m, grad, win, b_in, wout):
    rows, d = m.shape
    ff = win.shape[1]
    tf = 512
    cols = pl.BlockSpec((rows, tf), lambda i: (0, i))
    line = pl.BlockSpec((1, tf), lambda i: (0, i))
    return pl.pallas_call(
        mlp_kernel,
        grid=(ff // tf,),
        in_specs=[
            whole((rows, d)),
            whole((rows, d)),
            pl.BlockSpec((d, tf), lambda i: (0, i)),
            line,
            pl.BlockSpec((tf, d), lambda i: (i, 0)),
        ],
        out_specs=[whole((rows, d)), cols, cols, whole((rows, d)), line],
        out_shape=[
            jax.ShapeDtypeStruct((rows, d), F32),
            jax.ShapeDtypeStruct((rows, ff), BF16),
            jax.ShapeDtypeStruct((rows, ff), BF16),
            jax.ShapeDtypeStruct((rows, d), F32),
            jax.ShapeDtypeStruct((1, ff), F32),
        ],
        compiler_params=params(),
        cost_estimate=cost(8 * rows * d * ff, 4 * d * ff + 4 * rows * ff + 12 * rows * d, rows * ff * 2),
        name="mlp",
    )(m, grad, win, b_in, wout)


def one_hot(src_ref, n):
    return (lax.broadcasted_iota(jnp.int32, (src_ref.shape[0], n), 1) == src_ref[...]).astype(BF16)


def wgrad_kernel(src_ref, left_ref, right_ref, send_ref, keep_ref, bsum_ref, lt_ref):
    @pl.when(pl.program_id(0) == 0)
    def _():
        lt_ref[...] = dot_t(one_hot(src_ref, left_ref.shape[1]), left_ref[...]).astype(BF16)

    half = keep_ref.shape[0]
    right = right_ref[...]
    keep_ref[...] = dot(lt_ref[:half, :], right).astype(BF16)
    send_ref[...] = dot(lt_ref[half:, :], right).astype(BF16)
    bsum_ref[...] = jnp.sum(right.astype(F32), axis=0, keepdims=True)


def wgrad(src, left, right, c0, cols, tn=512):
    toks, d = left.shape
    out = pl.BlockSpec((d // 2, tn), lambda i: (0, i))
    return pl.pallas_call(
        wgrad_kernel,
        grid=(cols // tn,),
        in_specs=[
            whole((d, 1)),
            whole((toks, d)),
            pl.BlockSpec((toks, tn), lambda i: (0, c0 // tn + i)),
        ],
        out_specs=[out, out, pl.BlockSpec((1, tn), lambda i: (0, i))],
        out_shape=[jax.ShapeDtypeStruct((d // 2, cols), BF16)] * 2 + [jax.ShapeDtypeStruct((1, cols), F32)],
        scratch_shapes=[pltpu.VMEM((d, toks), BF16)],
        compiler_params=params(),
        cost_estimate=cost(2 * toks * d * (cols + d), 2 * toks * (d + cols) + 2 * d * cols),
        name="wgrad",
    )(src, left, right)


def wgrad_rows_kernel(half, n, tiles_ref, src_ref, left_ref, right_ref, send_ref, keep_ref):
    i = pl.program_id(0)
    lt = dot_t(one_hot(src_ref, left_ref.shape[1]), left_ref[...]).astype(BF16)
    out = dot(lt, right_ref[...]).astype(BF16)

    @pl.when(i < half)
    def _():
        send_ref[...] = out

    @pl.when(i >= half)
    def _():
        keep_ref[...] = out


def wgrad_rows(tiles, src, left, right):
    toks, d = right.shape
    n = tiles.shape[0]
    tile = left.shape[1] // n
    half = n // 2
    return pl.pallas_call(
        functools.partial(wgrad_rows_kernel, half, n),
        grid_spec=pltpu.PrefetchScalarGridSpec(
            num_scalar_prefetch=1,
            grid=(n,),
            in_specs=[
                pl.BlockSpec((tile, 1), lambda i, t: (0, 0)),
                pl.BlockSpec((toks, tile), lambda i, t: (0, t[i])),
                pl.BlockSpec((toks, d), lambda i, t: (0, 0)),
            ],
            out_specs=[
                pl.BlockSpec((tile, d), lambda i, t: (jnp.minimum(i, half - 1), 0)),
                pl.BlockSpec((tile, d), lambda i, t: (jnp.maximum(i - half, 0), 0)),
            ],
        ),
        out_shape=[jax.ShapeDtypeStruct((half * tile, d), BF16)] * 2,
        compiler_params=params(),
        cost_estimate=cost(2 * toks * n * tile * (d + tile), 2 * (n * tile * (d + toks) + toks * d)),
        name="wgrad_rows",
    )(tiles, src, left, right)


def back_kernel(a_ref, w_ref, out_ref, acc_ref):
    i = pl.program_id(0)

    @pl.when(i == 0)
    def _():
        acc_ref[...] = jnp.zeros_like(acc_ref)

    acc_ref[...] += dot_t(a_ref[...], w_ref[...])

    @pl.when(i == pl.num_programs(0) - 1)
    def _():
        out_ref[...] = acc_ref[...].astype(out_ref.dtype)


def back_product(a, w, piece, rows, dtype, tk=512, name="back"):
    d, depth = w.shape
    return pl.pallas_call(
        back_kernel,
        grid=(depth // tk,),
        in_specs=[
            pl.BlockSpec((rows, tk), lambda i: (piece, i)),
            pl.BlockSpec((d, tk), lambda i: (0, i)),
        ],
        out_specs=whole((rows, d)),
        out_shape=jax.ShapeDtypeStruct((rows, d), dtype),
        scratch_shapes=[pltpu.VMEM((rows, d), F32)],
        compiler_params=params(),
        cost_estimate=cost(2 * rows * d * depth, 2 * depth * (rows + d) + 4 * rows * d),
        name=name,
    )(a, w)


def join_kernel(x_ref, mlp_ref, ctx_ref, w_ref, bias_ref, out_ref):
    total = x_ref[...].astype(F32) + mlp_ref[...] + dot(ctx_ref[...], w_ref[...]) + bias_ref[...]
    out_ref[...] = total.astype(BF16)


def join(x, mlp_out, ctx, w, bias, tn=256):
    rows, d = x.shape
    cols = pl.BlockSpec((rows, tn), lambda i: (0, i))
    return pl.pallas_call(
        join_kernel,
        grid=(d // tn,),
        in_specs=[cols, cols, whole((rows, d)), pl.BlockSpec((d, tn), lambda i: (0, i)), pl.BlockSpec((1, tn), lambda i: (0, i))],
        out_specs=cols,
        out_shape=jax.ShapeDtypeStruct((rows, d), BF16),
        compiler_params=params(),
        cost_estimate=cost(2 * rows * d * d, 10 * rows * d + 2 * d * d),
        name="join",
    )(x, mlp_out, ctx, w, bias)


def lane_ids(rows):
    return lax.broadcasted_iota(jnp.int32, (rows, LANES), 1)


def swapped(x):
    h = ROT // 2
    lane = lane_ids(x.shape[0]) % HEAD
    return jnp.where(lane < h, pltpu.roll(x, LANES - h, 1), pltpu.roll(x, h, 1))


def qkv_kernel(a_ref, w_ref, bias_ref, cos_ref, sin_ref, q_ref, k_ref, v_ref):
    packed = dot(a_ref[...], w_ref[...]) + bias_ref[...]
    rows = packed.shape[0]
    first = lane_ids(rows) < HEAD
    pa, pb, pc = packed[:, :LANES], packed[:, LANES : 2 * LANES], packed[:, 2 * LANES :]
    q = jnp.where(first, pa, pb)
    k = pltpu.roll(jnp.where(first, pc, pa), HEAD, 1)
    v = jnp.where(first, pb, pc)
    cos, sin = cos_ref[...], sin_ref[...]
    q_ref[...] = (q * cos + swapped(q) * sin).astype(BF16)
    k_ref[...] = (k * cos + swapped(k) * sin).astype(BF16)
    v_ref[...] = v.astype(BF16)


def qkv(a, w, bias, cos, sin):
    rows, d = a.shape
    out = pl.BlockSpec((rows, LANES), lambda i: (0, i))
    return pl.pallas_call(
        qkv_kernel,
        grid=(w.shape[1] // PAIR,),
        in_specs=[
            whole((rows, d)),
            pl.BlockSpec((d, PAIR), lambda i: (0, i)),
            pl.BlockSpec((1, PAIR), lambda i: (0, i)),
            whole((rows, LANES)),
            whole((rows, LANES)),
        ],
        out_specs=[out] * 3,
        out_shape=[jax.ShapeDtypeStruct((rows, w.shape[1] // 3), BF16)] * 3,
        compiler_params=params(),
        cost_estimate=cost(2 * rows * d * w.shape[1], 8 * rows * d + 2 * d * w.shape[1]),
        name="qkv",
    )(a, w, bias, cos, sin)


def attention_kernel(
    toks,
    win,
    low_ref,
    start_ref,
    q_ref,
    k_ref,
    v_ref,
    do_ref,
    cos_ref,
    sin_ref,
    ctx_ref,
    dp_ref,
    k2,
    v2,
    kt,
    vt,
    s_ref,
    e_ref,
    dq_acc,
    dk_acc,
    dv_acc,
):
    nk = win // BLOCK
    halo = win - toks
    first = lane_ids(BLOCK) < HEAD
    zero = jnp.zeros((BLOCK, LANES), BF16)
    top = lax.broadcasted_iota(jnp.int32, (LANES, BLOCK), 0) < HEAD
    for j in range(nk):
        rows = slice(j * BLOCK, (j + 1) * BLOCK)
        for src, two, tr in ((k_ref, k2, kt), (v_ref, v2, vt)):
            x = src[rows, :]
            a, b = jnp.where(first, x, zero), jnp.where(first, zero, x)
            two[j, :BLOCK, :] = a
            two[j, BLOCK:, :] = b
            tr[j, :, :BLOCK] = a.astype(F32).T.astype(BF16)
            tr[j, :, BLOCK:] = b.astype(F32).T.astype(BF16)
    dk_acc[...] = jnp.zeros_like(dk_acc)
    dv_acc[...] = jnp.zeros_like(dv_acc)
    scale = HEAD**-0.5
    for i in range(toks // BLOCK):
        rows = slice(i * BLOCK, (i + 1) * BLOCK)
        last = halo // BLOCK + i
        low = low_ref[i]
        q = (q_ref[rows, :].astype(F32) * scale).astype(BF16)
        q0, q1 = jnp.where(first, q, zero), jnp.where(first, zero, q)
        start = start_ref[:, rows]
        q_at = halo + i * BLOCK + lax.broadcasted_iota(jnp.int32, (1, BLOCK), 1)

        def scores(j, peak):
            s = dot_t(k2[j], q)
            at = j * BLOCK + lax.broadcasted_iota(jnp.int32, (BLOCK, BLOCK), 0)
            ok = (at >= start) & (at <= q_at)
            s0 = jnp.where(ok, s[:BLOCK], NEG)
            s1 = jnp.where(ok, s[BLOCK:], NEG)
            s_ref[j, :BLOCK, :] = s0
            s_ref[j, BLOCK:, :] = s1
            return (
                jnp.maximum(peak[0], jnp.max(s0, axis=0, keepdims=True)),
                jnp.maximum(peak[1], jnp.max(s1, axis=0, keepdims=True)),
            )

        floor = jnp.full((1, BLOCK), NEG, F32)
        m0, m1 = lax.fori_loop(low, last + 1, scores, (floor, floor))

        def weigh(j, carry):
            t0, t1, acc = carry
            e0 = jnp.exp(s_ref[j, :BLOCK, :] - m0)
            e1 = jnp.exp(s_ref[j, BLOCK:, :] - m1)
            e_ref[j, :BLOCK, :] = e0.astype(BF16)
            e_ref[j, BLOCK:, :] = e1.astype(BF16)
            acc = acc + dot(vt[j], e_ref[j])
            return (
                t0 + jnp.sum(e0, axis=0, keepdims=True),
                t1 + jnp.sum(e1, axis=0, keepdims=True),
                acc,
            )

        none = jnp.zeros((1, BLOCK), F32)
        t0, t1, acc = lax.fori_loop(low, last + 1, weigh, (none, none, jnp.zeros((LANES, BLOCK), F32)))
        r0, r1 = 1.0 / t0, 1.0 / t1
        share = jnp.where(top, r0, r1)
        ctx_t = acc * share
        ctx_ref[rows, :] = ctx_t.T.astype(BF16)
        do_t = do_ref[rows, :].astype(F32).T * share
        both = do_t * ctx_t
        d0 = jnp.sum(jnp.where(top, both, 0.0), axis=0, keepdims=True)
        d1 = jnp.sum(jnp.where(top, 0.0, both), axis=0, keepdims=True)
        do = do_t.T.astype(BF16)
        do0, do1 = jnp.where(first, do, zero), jnp.where(first, zero, do)

        def back(j, dq):
            dp = dot_t(v2[j], do)
            e = e_ref[j]
            e0, e1 = e[:BLOCK], e[BLOCK:]
            ds0 = (e0.astype(F32) * (dp[:BLOCK] - d0)).astype(BF16)
            ds1 = (e1.astype(F32) * (dp[BLOCK:] - d1)).astype(BF16)
            at = pl.ds(pl.multiple_of(j * BLOCK, BLOCK), BLOCK)
            dk_acc[at, :] += dot(ds0, q0) + dot(ds1, q1)
            dv_acc[at, :] += dot(e0, do0) + dot(e1, do1)
            return dq + dot(kt[j, :, :BLOCK], ds0) + dot(kt[j, :, BLOCK:], ds1)

        dq_t = lax.fori_loop(low, last + 1, back, jnp.zeros((LANES, BLOCK), F32))
        dq_acc[rows, :] = dq_t.T * scale
    for j in range(nk):
        rows = slice(j * BLOCK, (j + 1) * BLOCK)
        cos, sin = cos_ref[rows, :], sin_ref[rows, :]
        dk = dk_acc[rows, :]
        dk = pltpu.roll(dk * cos - swapped(dk) * sin, HEAD, 1)
        dv = dv_acc[rows, :]
        if j * BLOCK >= halo:
            own = slice(j * BLOCK - halo, (j + 1) * BLOCK - halo)
            dq = dq_acc[own, :]
            dq = dq * cos - swapped(dq) * sin
        else:
            dq = jnp.zeros_like(dk)
        dp_ref[rows, :LANES] = jnp.where(first, dq, dk).astype(BF16)
        dp_ref[rows, LANES : 2 * LANES] = jnp.where(first, dv, dq).astype(BF16)
        dp_ref[rows, 2 * LANES :] = jnp.where(first, dk, dv).astype(BF16)


def attention(low, start, q, k, v, d_ctx, cos, sin):
    win, d = k.shape
    toks = d_ctx.shape[0]
    nk = win // BLOCK
    own = pl.BlockSpec((toks, LANES), lambda i, t: (0, i))
    own_q = pl.BlockSpec((toks, LANES), lambda i, t: (win // toks - 1, i))
    every = pl.BlockSpec((win, LANES), lambda i, t: (0, i))
    fixed = lambda shape: pl.BlockSpec(shape, lambda i, t: (0, 0))
    pairs = d // LANES
    return pl.pallas_call(
        functools.partial(attention_kernel, toks, win),
        grid_spec=pltpu.PrefetchScalarGridSpec(
            num_scalar_prefetch=1,
            grid=(pairs,),
            in_specs=[fixed((1, toks)), own_q, every, every, own, fixed((win, LANES)), fixed((win, LANES))],
            out_specs=[own, pl.BlockSpec((win, PAIR), lambda i, t: (0, i))],
            scratch_shapes=[
                pltpu.VMEM((nk, 2 * BLOCK, LANES), BF16),
                pltpu.VMEM((nk, 2 * BLOCK, LANES), BF16),
                pltpu.VMEM((nk, LANES, 2 * BLOCK), BF16),
                pltpu.VMEM((nk, LANES, 2 * BLOCK), BF16),
                pltpu.VMEM((nk, 2 * BLOCK, BLOCK), F32),
                pltpu.VMEM((nk, 2 * BLOCK, BLOCK), BF16),
                pltpu.VMEM((toks, LANES), F32),
                pltpu.VMEM((win, LANES), F32),
                pltpu.VMEM((win, LANES), F32),
            ],
        ),
        out_shape=[
            jax.ShapeDtypeStruct((toks, d), BF16),
            jax.ShapeDtypeStruct((win, 3 * d), BF16),
        ],
        compiler_params=params(),
        cost_estimate=cost(pairs * toks * DOC_MOST * 4 * 6 * LANES, 14 * win * d, pairs * 2 * toks * DOC_MOST),
        name="attention",
    )(low, start, q, k, v, d_ctx, cos, sin)


def shards(
    hidden_in,
    doc_lengths,
    ln1_gain,
    ln1_bias,
    ln2_gain,
    ln2_bias,
    qkv_weight,
    qkv_bias,
    dense_weight,
    dense_bias,
    fc_in_weight,
    fc_in_bias,
    fc_out_weight,
    fc_out_bias,
    out_grad,
):
    _, toks, d = hidden_in.shape
    ff = fc_in_weight.shape[1]
    ndp, nseq = lax.axis_size("dp"), lax.axis_size("seq")
    ndev = ndp * nseq
    sizes = {"dp": ndp, "seq": nseq}
    me_dp, me_seq = lax.axis_index("dp"), lax.axis_index("seq")
    row = lambda v: v.reshape(1, -1)

    halos = min(-(-(DOC_MOST - 1) // toks), nseq - 1)
    halos = max(halos, 1)
    win = (halos + 1) * toks
    base = (me_seq - halos) * toks
    lengths = doc_lengths.reshape(-1)
    docs = lengths.shape[0]
    order = jnp.arange(docs, dtype=jnp.int32)
    ends = jnp.sum(jnp.where(order[None, :] <= order[:, None], lengths[None, :], 0), axis=1)
    at = base + jnp.arange(win, dtype=jnp.int32)
    begin = jnp.max(jnp.where(at[:, None] >= ends[None, :], ends[None, :], 0), axis=1)
    doc_pos = at - begin
    live = (at[halos * toks :] < ends[docs - 2]).astype(F32).reshape(toks, 1)
    start = (begin - base)[halos * toks :]
    low = start[::BLOCK] // BLOCK
    lane = jnp.arange(LANES, dtype=jnp.int32) % HEAD
    half = ROT // 2
    freq = 10000.0 ** (-(2.0 * (lane % half).astype(F32)) / ROT)
    angle = doc_pos.astype(F32)[:, None] * freq[None, :]
    cos = jnp.where(lane < ROT, jnp.cos(angle), 1.0)
    sin = jnp.where(lane < half, -1.0, jnp.where(lane < ROT, 1.0, 0.0)) * jnp.sin(angle)

    x = hidden_in.reshape(toks, d)
    a_own, m_own, grad, grad_sum = norms(
        x, out_grad.reshape(toks, d), live, row(ln1_gain), row(ln1_bias), row(ln2_gain), row(ln2_bias)
    )

    ahead = [(i, i + 1) for i in range(nseq - 1)]
    behind = [(i + 1, i) for i in range(nseq - 1)]
    pieces = [a_own]
    for _ in range(halos):
        pieces.append(lax.ppermute(pieces[-1], "seq", ahead))
    mlp_out, act, d_pre, d_mlp, b_in_sum = mlp(m_own, grad, fc_in_weight, row(fc_in_bias), fc_out_weight)

    order_a, order_b = stage_order(ndp, nseq, False), stage_order(ndp, nseq, True)
    src_a = row_sources(d, order_a, ndp, nseq, me_dp, me_seq)
    src_b = row_sources(d, order_b, ndp, nseq, me_dp, me_seq)
    in_send, in_keep, _ = wgrad(src_a, m_own, d_pre, 0, ff)
    g_in = halving(in_send, in_keep, order_a, sizes)

    dp_bits = [b for axis, b in order_b if axis == "dp"]
    spots = jnp.arange(ndp, dtype=jnp.int32)
    tiles = me_dp ^ relative(jnp.where(spots < ndp // 2, spots + ndp // 2, spots - ndp // 2), dp_bits)
    src_t = row_sources(ff // ndp, [s for s in order_b if s[0] == "seq"], 1, nseq, 0, me_seq)
    out_send, out_keep = wgrad_rows(tiles, src_t, act, grad)
    g_out = halving(out_send, out_keep, order_b, sizes)

    d_ctx = back_product(grad, dense_weight, 0, toks, BF16, name="d_ctx")
    a_all = jnp.concatenate(pieces[::-1], axis=0)
    q, k, v = qkv(a_all, qkv_weight, row(qkv_bias), cos, sin)
    ctx, d_packed = attention(low, row(start), q, k, v, d_ctx, cos, sin)

    got = None
    for piece in range(halos):
        part = back_product(d_packed, qkv_weight, piece, toks, F32 if got is not None else BF16, name="d_attn")
        if got is not None:
            part = (part + got.astype(F32)).astype(BF16)
        got = lax.ppermute(part, "seq", behind)
    d_own = back_product(d_packed, qkv_weight, halos, toks, F32, name="d_attn")

    cut = 3 * d // 2
    qa_send, qa_keep, b_qkv_a = wgrad(src_a, a_all, d_packed, 0, cut)
    g_qkv_a = halving(qa_send, qa_keep, order_a, sizes)
    qb_send, qb_keep, b_qkv_b = wgrad(src_b, a_all, d_packed, cut, cut)
    g_qkv_b = halving(qb_send, qb_keep, order_b, sizes)
    de_send, de_keep, _ = wgrad(src_a, ctx, grad, 0, d)
    g_dense = halving(de_send, de_keep, order_a, sizes)

    hidden_out = join(x, mlp_out, ctx, dense_weight, row(dense_bias + fc_out_bias))
    grad_in, s1g, s1b, s2g, s2b = norm_back(x, grad, d_own, got, d_mlp, row(ln1_gain), row(ln2_gain))

    small = jnp.concatenate(
        [v.reshape(ndev, -1) for v in (s1g, s1b, s2g, s2b, grad_sum, b_qkv_a, b_qkv_b, b_in_sum)], axis=1
    )
    per = d // ndev
    b_qkv = jnp.concatenate([b_qkv_a, b_qkv_b], axis=1)
    small = jnp.concatenate(
        [v.reshape(ndev, -1) for v in (s1g, s1b, s2g, s2b, grad_sum, b_qkv, b_in_sum)], axis=1
    )
    small = lax.psum_scatter(small, ("dp", "seq"), scatter_dimension=0, tiled=True).reshape(-1)
    cuts = [per, 2 * per, 3 * per, 4 * per, 5 * per, 8 * per]
    o1g, o1b, o2g, o2b, o_db, o_qb, o_ib = jnp.split(small, cuts)
    g_qkv = jnp.concatenate([g_qkv_a, g_qkv_b], axis=1)
    return (
        hidden_out.reshape(hidden_in.shape),
        grad_in.reshape(hidden_in.shape),
        o1g,
        o1b,
        o2g,
        o2b,
        g_qkv,
        o_qb,
        g_dense,
        o_db,
        g_in,
        o_ib,
        g_out,
        o_db,
    )


def solution(mesh):
    both = P(("dp", "seq"))
    rows = P(("dp", "seq"), None)
    toks = P("dp", "seq", None)
    return jax.shard_map(
        shards,
        mesh=mesh,
        in_specs=(toks, P("dp", None)) + (P(),) * 12 + (toks,),
        out_specs=(toks, toks, both, both, both, both, rows, both, rows, both, rows, both, rows, both),
        check_vma=False,
    )
```

time: 1520 us -> 540 us (0.36)
  waiting for transfers between devices: 798 us -> 142 us
  matrix products: 211 us -> 0 us
  Pallas kernels: 0 us -> 186 us
  local copies, waits for them, and re-layouts: 160 us -> 22.5 us
  blocking collectives: 160 us -> 40.8 us
  other arithmetic: 156 us -> 47.8 us
  starting transfers between devices: 16.6 us -> 92.9 us
    reduce_scatter x4 -> x0, waiting for transfers between devices: 743 us -> none  [the longest x1 366 us: shards(): lax.psum_scatter(grad_terms[8], ('dp', 'seq'), scatter_dimension=0, tiled...]
    dot_general x36 -> x0, matrix products: 211 us -> none  [the longest x4 34.1 us: transpose_dot(): lax.dot_general(left, right, (((0,), (0,)), ((), ())), preferred_element_...]
    pallas_call x0 -> x15, Pallas kernels: none -> 186 us  [the longest x1 48 us: attention(): pl.pallas_call(functools.partial(attention_kernel, toks, win), grid_spec=...]
    ppermute x0 -> x29, waiting for transfers between devices: none -> 142 us  [the longest x25 124 us: halving(): lax.ppermute(send, axis, [(i, i ^ bit) for i in range(sizes[axis])])]
    all_to_all x1 -> x0, blocking collectives: 119 us -> none  [shards(): lax.all_to_all(d_heads, 'seq', split_axis=1, concat_axis=2, tiled=True)]
    ppermute x0 -> x29, starting transfers between devices: none -> 92.9 us  [the longest x25 81.5 us: halving(): lax.ppermute(send, axis, [(i, i ^ bit) for i in range(sizes[axis])])]
    unnamed x8 -> x0, other arithmetic: 89.7 us -> none
    all_to_all x3 -> x0, waiting for transfers between devices: 55.2 us -> none  [the longest x1 55.2 us: shards(): lax.all_to_all(turned, 'seq', split_axis=2, concat_axis=1, tiled=True)]
  transfers between devices with their start and end apart: 7 -> 29, of which waited for: 4 -> 13; matrix products, arithmetic and copies ran while one was open for 22% -> 9% of each run, Pallas kernels for 0% -> 34%
where the time goes in v1:
time: 540 us; the launch traced here: 533 us
  Pallas kernels  186 us (34%)
  waiting for transfers between devices  142 us (26%)
  starting transfers between devices  92.9 us (17%)
  other arithmetic  47.8 us (9%)
  blocking collectives  40.8 us (8%)
  local copies, waits for them, and re-layouts  22.5 us (4%)
    ppermute x25, waiting for transfers between devices, halving(): lax.ppermute(send, axis, [(i, i ^ bit) for i in range(sizes[axis])])  124 us
    ppermute x25, starting transfers between devices, halving(): lax.ppermute(send, axis, [(i, i ^ bit) for i in range(sizes[axis])])  81.5 us
    pallas_call x1, Pallas kernels, attention(): pl.pallas_call(functools.partial(attention_kernel, toks, win), grid_spec=...  48 us
    unnamed x1, blocking collectives  40.8 us
    pallas_call x4, Pallas kernels, wgrad(): pl.pallas_call(wgrad_kernel, grid=(cols // tn,), in_specs=[whole((d, 1)),...  37.8 us
    convert_element_type x20, other arithmetic, halving(): send = total.astype(BF16)  28.7 us
    pallas_call x4, Pallas kernels, back_product(): pl.pallas_call(back_kernel, grid=(depth // tk,), in_specs=[pl.BlockSpec((...  26.7 us
    pallas_call x1, Pallas kernels, qkv(): pl.pallas_call(qkv_kernel, grid=(w.shape[1] // PAIR,), in_specs=[whole((r...  24.2 us
  transfers between devices with their start and end apart: 29, of which 13 were waited for; matrix products, arithmetic and copies ran while one was open for 9% of the time, Pallas kernels for 34%

profile of v1, /device:TPU:0, one launch (start us, length us, event | category | flops | bytes accessed | tf_op | source)
XLA Modules:
  0.0 533.0 jit_solution(18035946739712542757)
XLA Ops:
  4.1 1.2 copy-done.14
  8.0 2.5 norms.1
  10.5 5.9 %collective-permute-start = (bf16[512,1024]{1,0:T(8,128)(2,1)}, bf16[512,1024]{1,0:T(8,128)(2,1)}, u32[]{:S(2)}, u32[]{:S(2)}) collective-permute-start(bf16[512,1024]{1,0:T(8,128)(2,1)} %get-tuple-element.48), channel_id=1, source_target_pairs={{0,1},{1,2},{2,3},{4,5},{5,6},{6,7},{8,9},{9,10},{10,11},{12,13},{... | collective-permute-start | bytes 3145736 | tf_op jit(solution)/shard_map/ppermute | solution.py:602
  16.5 1.5 fusion.13
  18.0 23.9 %mlp.1 = (f32[512,1024]{1,0:T(8,128)S(1)}, bf16[512,4096]{1,0:T(8,128)(2,1)}, bf16[512,4096]{1,0:T(8,128)(2,1)}, f32[512,1024]{1,0:T(8,128)}, f32[1,4096]{1,0:T(1,128)S(1)}) custom-call(bf16[512,1024]{1,0:T(8,128)(2,1)S(1)} %get-tuple-element.45.m_ref.left_ref, bf16[512,1024]{1,0:T(8,128)(2,1)S(1)} %get-tuple-element.46.grad_ref.a_ref.right_ref, ...), custom_call_target="tpu_custom_call" | custom-call | flops 17179869184 | bytes 31457280 | tf_op jit(solution)/shard_map/mlp/pallas_call | solution.py:190
  41.9 1.3 copy-done.5
  43.2 10.7 %wgrad.7 = (bf16[512,4096]{1,0:T(8,128)(2,1)}, bf16[512,4096]{1,0:T(8,128)(2,1)}, f32[1,4096]{1,0:T(1,128)}) custom-call(s32[1024,1]{1,0:T(8,128)S(1)} %get-tuple-element.83.src_ref, bf16[512,1024]{1,0:T(8,128)(2,1)S(1)} %get-tuple-element.45.m_ref.left_ref, bf16[512,4096]{1,0:T(8,128)(2,1)} %get-tuple-element.70.right_ref), custom_call_target="tpu_custom_call" | custom-call | flops 5368709120 | bytes 13631488 | tf_op jit(solution)/shard_map/wgrad/pallas_call | solution.py:233
  54.1 13.1 %wgrad_rows.1 = (bf16[2048,1024]{1,0:T(8,128)(2,1)}, bf16[2048,1024]{1,0:T(8,128)(2,1)}) custom-call(s32[8]{0:T(128)S(1)} %fusion.44.tiles_ref, s32[512,1]{1,0:T(8,128)S(1)} %fusion.33.src_ref, bf16[512,4096]{1,0:T(8,128)(2,1)} %get-tuple-element.73.left_ref, bf16[512,1024]{1,0:T(8,128)(2,1)S(1)} %get-tuple-element.46.grad_ref.a_ref.right_ref), custom_call_target="tpu_custom_call" | custom-call | flops 6442450944 | bytes 13631488 | tf_op jit(solution)/shard_map/wgrad_rows/pallas_call | solution.py:269
  69.2 2.7 collective-permute-start.1
  71.9 2.0 d_ctx.1.do_ref
  74.0 2.8 fusion.5
  76.8 17.8 %collective-permute-done.1 = bf16[512,1024]{1,0:T(8,128)(2,1)S(1)} collective-permute-done((bf16[512,1024]{1,0:T(8,128)(2,1)}, bf16[512,1024]{1,0:T(8,128)(2,1)S(1)}, u32[]{:S(2)}, u32[]{:S(2)}) %collective-permute-start.1) | collective-permute-done | bytes 1048608 | tf_op jit(solution)/shard_map/ppermute | solution.py:602
  94.7 1.3 constant_dynamic-update-slice_fusion.1
  96.0 1.3 constant_dynamic-update-slice_fusion.a_ref.left_ref
  97.3 1.7 copy-done.39
  99.0 24.2 %qkv.1 = (bf16[1536,1024]{1,0:T(8,128)(2,1)S(1)}, bf16[1536,1024]{1,0:T(8,128)(2,1)}, bf16[1536,1024]{1,0:T(8,128)(2,1)}) custom-call(bf16[1536,1024]{1,0:T(8,128)(2,1)} %copy-done.39, bf16[1024,3072]{1,0:T(8,128)(2,1)} %w_ref.11, f32[1,3072]{1,0:T(1,128)S(1)} %bitcast.44, f32[1536,128]{1,0:T(8,128)S(1)} %get-tuple-element.82.cos_ref, ...), custom_call_target="tpu_custom_call" | custom-call | flops 9663676416 | bytes 18874368 | tf_op jit(solution)/shard_map/qkv/pallas_call | solution.py:370
  123.2 1.7 copy-done.31
  124.9 48.0 %attention.1 = (bf16[512,1024]{1,0:T(8,128)(2,1)S(1)}, bf16[1536,3072]{1,0:T(8,128)(2,1)}) custom-call(s32[2]{0:T(128)S(1)} %and_select_fusion.2.low_ref, s32[1,512]{1,0:T(1,128)S(1)} %bitcast.42, bf16[1536,1024]{1,0:T(8,128)(2,1)} %copy-done.31, bf16[1536,1024]{1,0:T(8,128)(2,1)} %get-tuple-element.50.k_ref, bf16[1536,1024]{1,0:T(8,128)(2,1)} %get-tuple-element.51.v_ref, ...), custom_call_target="tpu_custom_call" | custom-call | flops 12884901888 | bytes 22020096 | tf_op jit(solution)/shard_map/attention/pallas_call | solution.py:518
  172.9 3.7 wgrad.6
  177.7 11.7 %wgrad.4 = (bf16[512,1536]{1,0:T(8,128)(2,1)S(1)}, bf16[512,1536]{1,0:T(8,128)(2,1)S(1)}, f32[1,1536]{1,0:T(1,128)S(1)}) custom-call(s32[1024,1]{1,0:T(8,128)S(1)} %copy-done.19, bf16[1536,1024]{1,0:T(8,128)(2,1)} %copy-done.39, bf16[1536,3072]{1,0:T(8,128)(2,1)} %get-tuple-element.53.a_ref.right_ref), custom_call_target="tpu_custom_call" | custom-call | flops 8053063680 | bytes 11010048 | tf_op jit(solution)/shard_map/wgrad/pallas_call | solution.py:233
  190.5 9.2 %d_attn.5 = bf16[512,1024]{1,0:T(8,128)(2,1)} custom-call(bf16[1536,3072]{1,0:T(8,128)(2,1)} %get-tuple-element.53.a_ref.right_ref, bf16[1024,3072]{1,0:T(8,128)(2,1)} %w_ref.11), custom_call_target="tpu_custom_call" | custom-call | flops 3221225472 | bytes 11534336 | tf_op jit(solution)/shard_map/d_attn/pallas_call | solution.py:307
  199.7 1.3 collective-permute-start.2
  201.0 11.7 %wgrad.5 = (bf16[512,1536]{1,0:T(8,128)(2,1)S(1)}, bf16[512,1536]{1,0:T(8,128)(2,1)S(1)}, f32[1,1536]{1,0:T(1,128)S(1)}) custom-call(s32[1024,1]{1,0:T(8,128)S(1)} %copy-done.17, bf16[1536,1024]{1,0:T(8,128)(2,1)} %copy-done.39, bf16[1536,3072]{1,0:T(8,128)(2,1)} %get-tuple-element.53.a_ref.right_ref), custom_call_target="tpu_custom_call" | custom-call | flops 8053063680 | bytes 11010048 | tf_op jit(solution)/shard_map/wgrad/pallas_call | solution.py:233
  215.6 1.2 copy-done.13
  216.9 4.6 join.1
  221.5 1.2 add_convert_fusion.9
  222.7 1.5 collective-permute-start.15
  224.3 7.7 %d_attn.4 = f32[512,1024]{1,0:T(8,128)S(1)} custom-call(bf16[1536,3072]{1,0:T(8,128)(2,1)} %get-tuple-element.53.a_ref.right_ref, bf16[1024,3072]{1,0:T(8,128)(2,1)} %w_ref.11), custom_call_target="tpu_custom_call" | custom-call | flops 3221225472 | bytes 11534336 | tf_op jit(solution)/shard_map/d_attn/pallas_call | solution.py:307
  232.0 7.8 %d_attn.3.da_ref = f32[512,1024]{1,0:T(8,128)S(1)} custom-call(bf16[1536,3072]{1,0:T(8,128)(2,1)} %get-tuple-element.53.a_ref.right_ref, bf16[1024,3072]{1,0:T(8,128)(2,1)} %w_ref.11), custom_call_target="tpu_custom_call" | custom-call | flops 3221225472 | bytes 11534336 | tf_op jit(solution)/shard_map/d_attn/pallas_call | solution.py:307
  241.0 22.5 %collective-permute-start.16 = (bf16[128,1024]{1,0:T(8,128)(2,1)S(1)}, bf16[128,1024]{1,0:T(8,128)(2,1)S(1)}, u32[]{:S(2)}, u32[]{:S(2)}) collective-permute-start(bf16[128,1024]{1,0:T(8,128)(2,1)S(1)} %add_convert_fusion.14), channel_id=1, source_target_pairs={{0,16},{4,20},{8,24},{12,28},{16,0},{20,4},{24,8},{28,12},{1,17},{... | collective-permute-start | bytes 786440 | tf_op jit(solution)/shard_map/ppermute | solution.py:85
  263.5 1.6 add_convert_fusion.4
  265.1 4.4 collective-permute-done.16
  269.5 1.5 collective-permute-start.3
  272.0 19.0 %collective-permute-start.17 = (bf16[64,1024]{1,0:T(8,128)(2,1)S(1)}, bf16[64,1024]{1,0:T(8,128)(2,1)S(1)}, u32[]{:S(2)}, u32[]{:S(2)}) collective-permute-start(bf16[64,1024]{1,0:T(8,128)(2,1)S(1)} %add_convert_fusion.17), channel_id=1, source_target_pairs={{0,1},{1,0},{2,3},{3,2},{4,5},{5,4},{6,7},{7,6},{8,9},{9,8},{10,11... | collective-permute-start | bytes 393224 | tf_op jit(solution)/shard_map/ppermute | solution.py:85
  292.2 23.6 %collective-permute-done.17 = bf16[64,1024]{1,0:T(8,128)(2,1)S(1)} collective-permute-done((bf16[64,1024]{1,0:T(8,128)(2,1)S(1)}, bf16[64,1024]{1,0:T(8,128)(2,1)S(1)}, u32[]{:S(2)}, u32[]{:S(2)}) %collective-permute-start.17) | collective-permute-done | bytes 131104 | tf_op jit(solution)/shard_map/ppermute | solution.py:85
  315.8 1.5 collective-permute-start.10
  318.2 19.4 %collective-permute-start.18 = (bf16[32,1024]{1,0:T(8,128)(2,1)S(1)}, bf16[32,1024]{1,0:T(8,128)(2,1)S(1)}, u32[]{:S(2)}, u32[]{:S(2)}) collective-permute-start(bf16[32,1024]{1,0:T(8,128)(2,1)S(1)} %add_convert_fusion.20), channel_id=1, source_target_pairs={{0,2},{1,3},{2,0},{3,1},{4,6},{5,7},{6,4},{7,5},{8,10},{9,11},{10,... | collective-permute-start | bytes 196616 | tf_op jit(solution)/shard_map/ppermute | solution.py:85
  339.8 1.5 convert_add_fusion.4
  341.4 3.7 add_convert_fusion.1
  345.2 4.8 norm_back.1
  353.0 40.8 %all-reduce = f32[32,384]{1,0:T(8,128)S(1)} all-reduce(f32[32,384]{1,0:T(8,128)S(1)} %concatenate.14), channel_id=2, replica_groups=mesh['dp'=8,'seq'=4] {'dp','seq'}, use_global_device_ids=true, to_apply=%region_2.3.clone | all-reduce | flops 12288 | bytes 98304
  394.5 2.2 collective-permute-start.20
  396.7 3.4 add_convert_fusion
  400.1 1.6 collective-permute-start.25
  404.6 1.5 add_convert_fusion.11
  406.2 44.0 %collective-permute-done.11 = bf16[128,1536]{1,0:T(8,128)(2,1)S(1)} collective-permute-done((bf16[128,1536]{1,0:T(8,128)(2,1)S(1)}, bf16[128,1536]{1,0:T(8,128)(2,1)S(1)}, u32[]{:S(2)}, u32[]{:S(2)}) %collective-permute-start.11) | collective-permute-done | bytes 393248 | tf_op jit(solution)/shard_map/ppermute | solution.py:85
  451.3 3.6 collective-permute-done.6
  456.0 1.4 collective-permute-done.12
  458.4 1.5 collective-permute-start.13
  459.8 2.4 collective-permute-done.7
  464.3 1.8 add_convert_fusion.3
  466.1 2.0 collective-permute-start.21
  470.7 1.9 add_convert_fusion.2
  472.6 3.0 collective-permute-start.26
  475.6 12.0 %collective-permute-done.21 = bf16[128,4096]{1,0:T(8,128)(2,1)S(1)} collective-permute-done((bf16[128,4096]{1,0:T(8,128)(2,1)S(1)}, bf16[128,4096]{1,0:T(8,128)(2,1)S(1)}, u32[]{:S(2)}, u32[]{:S(2)}) %collective-permute-start.21) | collective-permute-done | bytes 1048608 | tf_op jit(solution)/shard_map/ppermute | solution.py:85
  487.6 1.3 add_convert_fusion.8
  488.9 1.8 collective-permute-start.22
  491.5 6.5 %collective-permute-done.26 = bf16[512,1024]{1,0:T(8,128)(2,1)S(1)} collective-permute-done((bf16[512,1024]{1,0:T(8,128)(2,1)S(1)}, bf16[512,1024]{1,0:T(8,128)(2,1)S(1)}, u32[]{:S(2)}, u32[]{:S(2)}) %collective-permute-start.26) | collective-permute-done | bytes 1048608 | tf_op jit(solution)/shard_map/ppermute | solution.py:85
  497.9 1.4 add_convert_fusion.7
  500.6 2.2 collective-permute-start.23
  502.8 14.5 %collective-permute-done.27 = bf16[256,1024]{1,0:T(8,128)(2,1)S(1)} collective-permute-done((bf16[256,1024]{1,0:T(8,128)(2,1)S(1)}, bf16[256,1024]{1,0:T(8,128)(2,1)S(1)}, u32[]{:S(2)}, u32[]{:S(2)}) %collective-permute-start.27) | collective-permute-done | bytes 524320 | tf_op jit(solution)/shard_map/ppermute | solution.py:85
  518.5 1.9 convert_add_fusion.1
  520.5 9.6 %collective-permute-done.28 = bf16[128,1024]{1,0:T(8,128)(2,1)S(1)} collective-permute-done((bf16[128,1024]{1,0:T(8,128)(2,1)S(1)}, bf16[128,1024]{1,0:T(8,128)(2,1)S(1)}, u32[]{:S(2)}, u32[]{:S(2)}) %collective-permute-start.28) | collective-permute-done | bytes 262176 | tf_op jit(solution)/shard_map/ppermute | solution.py:85
  530.0 2.0 convert_add_fusion
  (161 shorter events, 38.1 us)
Async XLA Ops:
  0.6 17.3 %copy-start.29 = (f32[4096]{0:T(1024)S(1)}, f32[4096]{0:T(1024)}, u32[]{:S(2)}) copy-start(f32[4096]{0:T(1024)} %param.26) | copy-start | bytes 49156
  2.8 1.2 copy-start
  4.1 1.2 copy-start.14
  10.5 162.4 %copy-start.3 = (bf16[512,1024]{1,0:T(8,128)(2,1)}, bf16[512,1024]{1,0:T(8,128)(2,1)S(1)}, u32[]{:S(2)}) copy-start(bf16[512,1024]{1,0:T(8,128)(2,1)S(1)} %get-tuple-element.46.grad_ref.a_ref.right_ref) | copy-start | bytes 3145732
  10.5 58.7 %collective-permute-start = (bf16[512,1024]{1,0:T(8,128)(2,1)}, bf16[512,1024]{1,0:T(8,128)(2,1)}, u32[]{:S(2)}, u32[]{:S(2)}) collective-permute-start(bf16[512,1024]{1,0:T(8,128)(2,1)} %get-tuple-element.48), channel_id=1, source_target_pairs={{0,1},{1,2},{2,3},{4,5},{5,6},{6,7},{8,9},{9,10},{10,11},{12,13},{... | collective-permute-start | bytes 3145736 | tf_op jit(solution)/shard_map/ppermute | solution.py:602
  18.0 25.3 %copy-start.18 = (s32[1024,1]{1,0:T(8,128)}, s32[1024,1]{1,0:T(8,128)S(1)}, u32[]{:S(2)}) copy-start(s32[1024,1]{1,0:T(8,128)S(1)} %get-tuple-element.83.src_ref) | copy-start | bytes 12292
  41.9 1.3 copy-start.5
  53.9 287.5 %collective-permute-start.19 = (bf16[512,4096]{1,0:T(8,128)(2,1)}, bf16[512,4096]{1,0:T(8,128)(2,1)}, u32[]{:S(2)}, u32[]{:S(2)}) collective-permute-start(bf16[512,4096]{1,0:T(8,128)(2,1)} %get-tuple-element.72), channel_id=1, source_target_pairs={{0,4},{4,0},{8,12},{12,8},{16,20},{20,16},{24,28},{28,24},{1,5},{5... | collective-permute-start | bytes 12582920 | tf_op jit(solution)/shard_map/ppermute | solution.py:85
  54.1 15.1 %copy-start.40 = (f32[1024]{0:T(1024)S(1)}, f32[1024]{0:T(1024)}, u32[]{:S(2)}) copy-start(f32[1024]{0:T(1024)} %param.24) | copy-start | bytes 12292
  54.1 15.1 %copy-start.41 = (f32[1024]{0:T(1024)S(1)}, f32[1024]{0:T(1024)}, u32[]{:S(2)}) copy-start(f32[1024]{0:T(1024)} %param.28) | copy-start | bytes 12292
  54.1 17.8 %copy-start.2 = (bf16[1024,1024]{1,0:T(8,128)(2,1)S(1)}, bf16[1024,1024]{1,0:T(8,128)(2,1)}, u32[]{:S(2)}) copy-start(bf16[1024,1024]{1,0:T(8,128)(2,1)} %w_ref.8) | copy-start | bytes 6291460
  67.2 329.5 %collective-permute-start.24 = (bf16[2048,1024]{1,0:T(8,128)(2,1)}, bf16[2048,1024]{1,0:T(8,128)(2,1)}, u32[]{:S(2)}, u32[]{:S(2)}) collective-permute-start(bf16[2048,1024]{1,0:T(8,128)(2,1)} %get-tuple-element.75), channel_id=1, source_target_pairs={{0,4},{4,0},{8,12},{12,8},{16,20},{20,16},{24,28},{28,24},{1,5},{5... | collective-permute-start | bytes 12582920 | tf_op jit(solution)/shard_map/ppermute | solution.py:85
  69.2 25.4 %collective-permute-start.1 = (bf16[512,1024]{1,0:T(8,128)(2,1)}, bf16[512,1024]{1,0:T(8,128)(2,1)S(1)}, u32[]{:S(2)}, u32[]{:S(2)}) collective-permute-start(bf16[512,1024]{1,0:T(8,128)(2,1)} %collective-permute-done), channel_id=1, source_target_pairs={{0,1},{1,2},{2,3},{4,5},{5,6},{6,7},{8,9},{9,10},{10,11},{12,13},{... | collective-permute-start | bytes 3145736 | tf_op jit(solution)/shard_map/ppermute | solution.py:602
  94.7 4.3 copy-start.30
  97.3 1.7 copy-start.39
  123.2 1.7 copy-start.31
  124.9 48.0 %copy-start.19 = (s32[1024,1]{1,0:T(8,128)S(1)}, s32[1024,1]{1,0:T(8,128)}, u32[]{:S(2)}) copy-start(s32[1024,1]{1,0:T(8,128)} %copy-done.18) | copy-start | bytes 12292
  172.9 3.8 copy-start.12
  177.6 43.8 %collective-permute-start.14 = (bf16[512,1024]{1,0:T(8,128)(2,1)}, bf16[512,1024]{1,0:T(8,128)(2,1)}, u32[]{:S(2)}, u32[]{:S(2)}) collective-permute-start(bf16[512,1024]{1,0:T(8,128)(2,1)} %get-tuple-element.69), channel_id=1, source_target_pairs={{0,4},{4,0},{8,12},{12,8},{16,20},{20,16},{24,28},{28,24},{1,5},{5... | collective-permute-start | bytes 3145736 | tf_op jit(solution)/shard_map/ppermute | solution.py:85
  190.5 9.2 %copy-start.7 = (bf16[512,1536]{1,0:T(8,128)(2,1)}, bf16[512,1536]{1,0:T(8,128)(2,1)S(1)}, u32[]{:S(2)}) copy-start(bf16[512,1536]{1,0:T(8,128)(2,1)S(1)} %get-tuple-element.64) | copy-start | bytes 4718596
  190.5 10.5 %copy-start.17 = (s32[1024,1]{1,0:T(8,128)S(1)}, s32[1024,1]{1,0:T(8,128)}, u32[]{:S(2)}) copy-start(s32[1024,1]{1,0:T(8,128)} %get-tuple-element.84.src_ref) | copy-start | bytes 12292
  199.7 41.3 %collective-permute-start.2 = (bf16[512,1024]{1,0:T(8,128)(2,1)}, bf16[512,1024]{1,0:T(8,128)(2,1)}, u32[]{:S(2)}, u32[]{:S(2)}) collective-permute-start(bf16[512,1024]{1,0:T(8,128)(2,1)} %d_attn.5), channel_id=1, source_target_pairs={{1,0},{2,1},{3,2},{5,4},{6,5},{7,6},{9,8},{10,9},{11,10},{13,12},{... | collective-permute-start | bytes 3145736 | tf_op jit(solution)/shard_map/ppermute | solution.py:628
  201.0 14.6 %copy-start.1 = (bf16[1,512,1024]{2,1,0:T(8,128)(2,1)S(1)}, bf16[1,512,1024]{2,1,0:T(8,128)(2,1)}, u32[]{:S(2)}) copy-start(bf16[1,512,1024]{2,1,0:T(8,128)(2,1)} %param.15) | copy-start | bytes 3145732
  201.0 14.6 %copy-start.6 = (f32[512,1024]{1,0:T(8,128)S(1)}, f32[512,1024]{1,0:T(8,128)}, u32[]{:S(2)}) copy-start(f32[512,1024]{1,0:T(8,128)} %copy-done.5) | copy-start | bytes 6291460
  215.1 56.9 %collective-permute-start.9 = (bf16[512,1536]{1,0:T(8,128)(2,1)}, bf16[512,1536]{1,0:T(8,128)(2,1)S(1)}, u32[]{:S(2)}, u32[]{:S(2)}) collective-permute-start(bf16[512,1536]{1,0:T(8,128)(2,1)} %copy-done.28), channel_id=1, source_target_pairs={{0,4},{4,0},{8,12},{12,8},{16,20},{20,16},{24,28},{28,24},{1,5},{5... | collective-permute-start | bytes 4718600 | tf_op jit(solution)/shard_map/ppermute | solution.py:85
  215.6 1.2 copy-start.13
  216.9 4.6 copy-start.16
  222.7 17.1 %collective-permute-start.15 = (bf16[256,1024]{1,0:T(8,128)(2,1)S(1)}, bf16[256,1024]{1,0:T(8,128)(2,1)S(1)}, u32[]{:S(2)}, u32[]{:S(2)}) collective-permute-start(bf16[256,1024]{1,0:T(8,128)(2,1)S(1)} %add_convert_fusion.9), channel_id=1, source_target_pairs={{0,8},{4,12},{8,0},{12,4},{16,24},{20,28},{24,16},{28,20},{1,9},{5... | collective-permute-start | bytes 1572872 | tf_op jit(solution)/shard_map/ppermute | solution.py:85
  232.0 7.8 %copy-start.27 = (bf16[512,1536]{1,0:T(8,128)(2,1)S(1)}, bf16[512,1536]{1,0:T(8,128)(2,1)}, u32[]{:S(2)}) copy-start(bf16[512,1536]{1,0:T(8,128)(2,1)} %copy-done.26) | copy-start | bytes 4718596
  239.8 78.4 %collective-permute-start.4 = (bf16[512,1536]{1,0:T(8,128)(2,1)S(1)}, bf16[512,1536]{1,0:T(8,128)(2,1)S(1)}, u32[]{:S(2)}, u32[]{:S(2)}) collective-permute-start(bf16[512,1536]{1,0:T(8,128)(2,1)S(1)} %copy-done.27), channel_id=1, source_target_pairs={{0,4},{4,0},{8,12},{12,8},{16,20},{20,16},{24,28},{28,24},{1,5},{5... | collective-permute-start | bytes 4718600 | tf_op jit(solution)/shard_map/ppermute | solution.py:85
  241.0 50.1 %copy-start.10 = (bf16[512,1536]{1,0:T(8,128)(2,1)S(1)}, bf16[512,1536]{1,0:T(8,128)(2,1)}, u32[]{:S(2)}) copy-start(bf16[512,1536]{1,0:T(8,128)(2,1)} %copy-done.9) | copy-start | bytes 4718596
  241.0 28.5 %collective-permute-start.16 = (bf16[128,1024]{1,0:T(8,128)(2,1)S(1)}, bf16[128,1024]{1,0:T(8,128)(2,1)S(1)}, u32[]{:S(2)}, u32[]{:S(2)}) collective-permute-start(bf16[128,1024]{1,0:T(8,128)(2,1)S(1)} %add_convert_fusion.14), channel_id=1, source_target_pairs={{0,16},{4,20},{8,24},{12,28},{16,0},{20,4},{24,8},{28,12},{1,17},{... | collective-permute-start | bytes 786440 | tf_op jit(solution)/shard_map/ppermute | solution.py:85
  265.1 72.5 %copy-start.8 = (bf16[512,1536]{1,0:T(8,128)(2,1)S(1)}, bf16[512,1536]{1,0:T(8,128)(2,1)}, u32[]{:S(2)}) copy-start(bf16[512,1536]{1,0:T(8,128)(2,1)} %copy-done.7) | copy-start | bytes 4718596
  269.5 75.7 %collective-permute-start.3 = (bf16[512,1024]{1,0:T(8,128)(2,1)S(1)}, bf16[512,1024]{1,0:T(8,128)(2,1)S(1)}, u32[]{:S(2)}, u32[]{:S(2)}) collective-permute-start(bf16[512,1024]{1,0:T(8,128)(2,1)S(1)} %add_convert_fusion.4), channel_id=1, source_target_pairs={{1,0},{2,1},{3,2},{5,4},{6,5},{7,6},{9,8},{10,9},{11,10},{13,12},{... | collective-permute-start | bytes 3145736 | tf_op jit(solution)/shard_map/ppermute | solution.py:628
  272.0 66.7 %copy-start.35 = (bf16[512,1536]{1,0:T(8,128)(2,1)}, bf16[512,1536]{1,0:T(8,128)(2,1)S(1)}, u32[]{:S(2)}) copy-start(bf16[512,1536]{1,0:T(8,128)(2,1)S(1)} %collective-permute-done.9) | copy-start | bytes 4718596
  272.0 43.7 %collective-permute-start.17 = (bf16[64,1024]{1,0:T(8,128)(2,1)S(1)}, bf16[64,1024]{1,0:T(8,128)(2,1)S(1)}, u32[]{:S(2)}, u32[]{:S(2)}) collective-permute-start(bf16[64,1024]{1,0:T(8,128)(2,1)S(1)} %add_convert_fusion.17), channel_id=1, source_target_pairs={{0,1},{1,0},{2,3},{3,2},{4,5},{5,4},{6,7},{7,6},{8,9},{9,8},{10,11... | collective-permute-start | bytes 393224 | tf_op jit(solution)/shard_map/ppermute | solution.py:85
  291.1 50.3 %copy-start.32 = (bf16[512,4096]{1,0:T(8,128)(2,1)S(1)}, bf16[512,4096]{1,0:T(8,128)(2,1)}, u32[]{:S(2)}) copy-start(bf16[512,4096]{1,0:T(8,128)(2,1)} %get-tuple-element.71) | copy-start | bytes 12582916
  315.8 87.0 %collective-permute-start.10 = (bf16[256,1536]{1,0:T(8,128)(2,1)}, bf16[256,1536]{1,0:T(8,128)(2,1)}, u32[]{:S(2)}, u32[]{:S(2)}) collective-permute-start(bf16[256,1536]{1,0:T(8,128)(2,1)} %add_convert_fusion.5), channel_id=1, source_target_pairs={{0,16},{4,20},{8,24},{12,28},{16,0},{20,4},{24,8},{28,12},{1,17},{... | collective-permute-start | bytes 2359304 | tf_op jit(solution)/shard_map/ppermute | solution.py:85
  318.2 23.2 %copy-start.37 = (bf16[512,1536]{1,0:T(8,128)(2,1)}, bf16[512,1536]{1,0:T(8,128)(2,1)S(1)}, u32[]{:S(2)}) copy-start(bf16[512,1536]{1,0:T(8,128)(2,1)S(1)} %collective-permute-done.4) | copy-start | bytes 4718596
  318.2 21.6 %collective-permute-start.18 = (bf16[32,1024]{1,0:T(8,128)(2,1)S(1)}, bf16[32,1024]{1,0:T(8,128)(2,1)S(1)}, u32[]{:S(2)}, u32[]{:S(2)}) collective-permute-start(bf16[32,1024]{1,0:T(8,128)(2,1)S(1)} %add_convert_fusion.20), channel_id=1, source_target_pairs={{0,2},{1,3},{2,0},{3,1},{4,6},{5,7},{6,4},{7,5},{8,10},{9,11},{10,... | collective-permute-start | bytes 196616 | tf_op jit(solution)/shard_map/ppermute | solution.py:85
  339.8 64.8 %collective-permute-start.5 = (bf16[256,1536]{1,0:T(8,128)(2,1)}, bf16[256,1536]{1,0:T(8,128)(2,1)}, u32[]{:S(2)}, u32[]{:S(2)}) collective-permute-start(bf16[256,1536]{1,0:T(8,128)(2,1)} %add_convert_fusion.6), channel_id=1, source_target_pairs={{0,8},{4,12},{8,0},{12,4},{16,24},{20,28},{24,16},{28,20},{1,9},{5... | collective-permute-start | bytes 2359304 | tf_op jit(solution)/shard_map/ppermute | solution.py:85
  341.4 3.8 copy-start.4
  341.4 3.8 copy-start.21
  341.4 3.8 copy-start.23
  394.5 137.6 %copy-start.42 = (f32[32]{0:T(128)}, f32[32]{0:T(128)S(1)}, u32[]{:S(2)}) copy-start(f32[32]{0:T(128)S(1)} %get-tuple-element.114) | copy-start | bytes 388
  394.5 69.8 %collective-permute-start.20 = (bf16[256,4096]{1,0:T(8,128)(2,1)}, bf16[256,4096]{1,0:T(8,128)(2,1)S(1)}, u32[]{:S(2)}, u32[]{:S(2)}) collective-permute-start(bf16[256,4096]{1,0:T(8,128)(2,1)} %add_convert_fusion.1), channel_id=1, source_target_pairs={{0,8},{4,12},{8,0},{12,4},{16,24},{20,28},{24,16},{28,20},{1,9},{5... | collective-permute-start | bytes 6291464 | tf_op jit(solution)/shard_map/ppermute | solution.py:85
  396.7 6.1 %copy-start.11 = (bf16[512,1536]{1,0:T(8,128)(2,1)S(1)}, bf16[512,1536]{1,0:T(8,128)(2,1)}, u32[]{:S(2)}) copy-start(bf16[512,1536]{1,0:T(8,128)(2,1)} %copy-done.9) | copy-start | bytes 4718596
  396.7 6.1 %copy-start.36 = (bf16[512,1536]{1,0:T(8,128)(2,1)S(1)}, bf16[512,1536]{1,0:T(8,128)(2,1)}, u32[]{:S(2)}) copy-start(bf16[512,1536]{1,0:T(8,128)(2,1)} %copy-done.35) | copy-start | bytes 4718596
  396.7 7.9 %copy-start.38 = (bf16[512,1536]{1,0:T(8,128)(2,1)S(1)}, bf16[512,1536]{1,0:T(8,128)(2,1)}, u32[]{:S(2)}) copy-start(bf16[512,1536]{1,0:T(8,128)(2,1)} %copy-done.37) | copy-start | bytes 4718596
  400.1 70.6 %collective-permute-start.25 = (bf16[1024,1024]{1,0:T(8,128)(2,1)S(1)}, bf16[1024,1024]{1,0:T(8,128)(2,1)S(1)}, u32[]{:S(2)}, u32[]{:S(2)}) collective-permute-start(bf16[1024,1024]{1,0:T(8,128)(2,1)S(1)} %add_convert_fusion), channel_id=1, source_target_pairs={{0,16},{4,20},{8,24},{12,28},{16,0},{20,4},{24,8},{28,12},{1,17},{... | collective-permute-start | bytes 6291464 | tf_op jit(solution)/shard_map/ppermute | solution.py:85
  403.9 60.4 %copy-start.33 = (bf16[512,4096]{1,0:T(8,128)(2,1)S(1)}, bf16[512,4096]{1,0:T(8,128)(2,1)}, u32[]{:S(2)}) copy-start(bf16[512,4096]{1,0:T(8,128)(2,1)} %get-tuple-element.71) | copy-start | bytes 12582916
  404.0 46.2 %collective-permute-start.11 = (bf16[128,1536]{1,0:T(8,128)(2,1)S(1)}, bf16[128,1536]{1,0:T(8,128)(2,1)S(1)}, u32[]{:S(2)}, u32[]{:S(2)}) collective-permute-start(bf16[128,1536]{1,0:T(8,128)(2,1)S(1)} %add_convert_fusion.10), channel_id=1, source_target_pairs={{0,8},{4,12},{8,0},{12,4},{16,24},{20,28},{24,16},{28,20},{1,9},{5... | collective-permute-start | bytes 1179656 | tf_op jit(solution)/shard_map/ppermute | solution.py:85
  406.1 48.8 %collective-permute-start.6 = (bf16[128,1536]{1,0:T(8,128)(2,1)S(1)}, bf16[128,1536]{1,0:T(8,128)(2,1)S(1)}, u32[]{:S(2)}, u32[]{:S(2)}) collective-permute-start(bf16[128,1536]{1,0:T(8,128)(2,1)S(1)} %add_convert_fusion.11), channel_id=1, source_target_pairs={{0,16},{4,20},{8,24},{12,28},{16,0},{20,4},{24,8},{28,12},{1,17},{... | collective-permute-start | bytes 1179656 | tf_op jit(solution)/shard_map/ppermute | solution.py:85
  451.2 6.2 %collective-permute-start.12 = (bf16[64,1536]{1,0:T(8,128)(2,1)S(1)}, bf16[64,1536]{1,0:T(8,128)(2,1)S(1)}, u32[]{:S(2)}, u32[]{:S(2)}) collective-permute-start(bf16[64,1536]{1,0:T(8,128)(2,1)S(1)} %add_convert_fusion.15), channel_id=1, source_target_pairs={{0,1},{1,0},{2,3},{3,2},{4,5},{5,4},{6,7},{7,6},{8,9},{9,8},{10,11... | collective-permute-start | bytes 589832 | tf_op jit(solution)/shard_map/ppermute | solution.py:85
  455.9 6.3 %collective-permute-start.7 = (bf16[64,1536]{1,0:T(8,128)(2,1)S(1)}, bf16[64,1536]{1,0:T(8,128)(2,1)S(1)}, u32[]{:S(2)}, u32[]{:S(2)}) collective-permute-start(bf16[64,1536]{1,0:T(8,128)(2,1)S(1)} %add_convert_fusion.16), channel_id=1, source_target_pairs={{0,1},{1,0},{2,3},{3,2},{4,5},{5,4},{6,7},{7,6},{8,9},{9,8},{10,11... | collective-permute-start | bytes 589832 | tf_op jit(solution)/shard_map/ppermute | solution.py:85
  458.4 9.8 %collective-permute-start.13 = (bf16[32,1536]{1,0:T(8,128)(2,1)S(1)}, bf16[32,1536]{1,0:T(8,128)(2,1)S(1)}, u32[]{:S(2)}, u32[]{:S(2)}) collective-permute-start(bf16[32,1536]{1,0:T(8,128)(2,1)S(1)} %add_convert_fusion.18), channel_id=1, source_target_pairs={{0,2},{1,3},{2,0},{3,1},{4,6},{5,7},{6,4},{7,5},{8,10},{9,11},{10,... | collective-permute-start | bytes 294920 | tf_op jit(solution)/shard_map/ppermute | solution.py:85
  463.2 7.5 %copy-start.34 = (bf16[2048,1024]{1,0:T(8,128)(2,1)S(1)}, bf16[2048,1024]{1,0:T(8,128)(2,1)}, u32[]{:S(2)}) copy-start(bf16[2048,1024]{1,0:T(8,128)(2,1)} %get-tuple-element.74) | copy-start | bytes 12582916
  463.2 6.6 %collective-permute-start.8 = (bf16[32,1536]{1,0:T(8,128)(2,1)S(1)}, bf16[32,1536]{1,0:T(8,128)(2,1)S(1)}, u32[]{:S(2)}, u32[]{:S(2)}) collective-permute-start(bf16[32,1536]{1,0:T(8,128)(2,1)S(1)} %add_convert_fusion.19), channel_id=1, source_target_pairs={{0,2},{1,3},{2,0},{3,1},{4,6},{5,7},{6,4},{7,5},{8,10},{9,11},{10,... | collective-permute-start | bytes 294920 | tf_op jit(solution)/shard_map/ppermute | solution.py:85
  466.1 21.4 %collective-permute-start.21 = (bf16[128,4096]{1,0:T(8,128)(2,1)S(1)}, bf16[128,4096]{1,0:T(8,128)(2,1)S(1)}, u32[]{:S(2)}, u32[]{:S(2)}) collective-permute-start(bf16[128,4096]{1,0:T(8,128)(2,1)S(1)} %add_convert_fusion.3), channel_id=1, source_target_pairs={{0,16},{4,20},{8,24},{12,28},{16,0},{20,4},{24,8},{28,12},{1,17},{... | collective-permute-start | bytes 3145736 | tf_op jit(solution)/shard_map/ppermute | solution.py:85
  472.6 25.4 %collective-permute-start.26 = (bf16[512,1024]{1,0:T(8,128)(2,1)S(1)}, bf16[512,1024]{1,0:T(8,128)(2,1)S(1)}, u32[]{:S(2)}, u32[]{:S(2)}) collective-permute-start(bf16[512,1024]{1,0:T(8,128)(2,1)S(1)} %add_convert_fusion.2), channel_id=1, source_target_pairs={{0,8},{4,12},{8,0},{12,4},{16,24},{20,28},{24,16},{28,20},{1,9},{5... | collective-permute-start | bytes 3145736 | tf_op jit(solution)/shard_map/ppermute | solution.py:85
  488.9 10.6 %collective-permute-start.22 = (bf16[64,4096]{1,0:T(8,128)(2,1)S(1)}, bf16[64,4096]{1,0:T(8,128)(2,1)S(1)}, u32[]{:S(2)}, u32[]{:S(2)}) collective-permute-start(bf16[64,4096]{1,0:T(8,128)(2,1)S(1)} %add_convert_fusion.8), channel_id=1, source_target_pairs={{0,1},{1,0},{2,3},{3,2},{4,5},{5,4},{6,7},{7,6},{8,9},{9,8},{10,11... | collective-permute-start | bytes 1572872 | tf_op jit(solution)/shard_map/ppermute | solution.py:85
  499.4 17.9 %collective-permute-start.27 = (bf16[256,1024]{1,0:T(8,128)(2,1)S(1)}, bf16[256,1024]{1,0:T(8,128)(2,1)S(1)}, u32[]{:S(2)}, u32[]{:S(2)}) collective-permute-start(bf16[256,1024]{1,0:T(8,128)(2,1)S(1)} %add_convert_fusion.7), channel_id=1, source_target_pairs={{0,1},{1,0},{2,3},{3,2},{4,5},{5,4},{6,7},{7,6},{8,9},{9,8},{10,11... | collective-permute-start | bytes 1572872 | tf_op jit(solution)/shard_map/ppermute | solution.py:85
  500.6 18.0 %collective-permute-start.23 = (bf16[32,4096]{1,0:T(8,128)(2,1)S(1)}, bf16[32,4096]{1,0:T(8,128)(2,1)S(1)}, u32[]{:S(2)}, u32[]{:S(2)}) collective-permute-start(bf16[32,4096]{1,0:T(8,128)(2,1)S(1)} %add_convert_fusion.13), channel_id=1, source_target_pairs={{0,2},{1,3},{2,0},{3,1},{4,6},{5,7},{6,4},{7,5},{8,10},{9,11},{10,... | collective-permute-start | bytes 786440 | tf_op jit(solution)/shard_map/ppermute | solution.py:85
  518.4 11.6 %collective-permute-start.28 = (bf16[128,1024]{1,0:T(8,128)(2,1)S(1)}, bf16[128,1024]{1,0:T(8,128)(2,1)S(1)}, u32[]{:S(2)}, u32[]{:S(2)}) collective-permute-start(bf16[128,1024]{1,0:T(8,128)(2,1)S(1)} %add_convert_fusion.12), channel_id=1, source_target_pairs={{0,2},{1,3},{2,0},{3,1},{4,6},{5,7},{6,4},{7,5},{8,10},{9,11},{10,... | collective-permute-start | bytes 786440 | tf_op jit(solution)/shard_map/ppermute | solution.py:85
  (8 other events, 7.2 us)
